TPU v7x, 256 devices: a whole 4x4x8 slice. The times are simulated.
256 devices in a mesh: tile: 64 (over z, x, core), samp: 4 (over y).
Axes of the slice: x: 4, y: 4, z: 8, core: 2. Of those that a mesh axis runs over, the one named last changes fastest.
Arguments:
- samples_w: bfloat16 [65536, 1024], P('tile', 'samp'), may hold values from -6 to 6
- dense_tiles: bfloat16 [65536, 1024], P(('tile', 'samp')), may hold values from -0.1875 to 0.1875
- left_factors: bfloat16 [65536, 2048], P('tile'), may hold values from -0.125 to 0.125
- right_factors: bfloat16 [65536, 2048], P('tile'), may hold values from -0.1875 to 0.1875
- ranks: int32 [64, 64], P(None, 'tile'), may hold values from 8 to 32
- area_blocks: bfloat16 [65536, 1024], P('tile'), may hold values from -0.03125 to 0.03125
- area_group: int32 [64], P('tile'), may hold values from 0 to 1
- counts: int32 [2048], replicated, may hold values from 0 to 5
Outputs:
- area_grad: bfloat16 [2048, 1024], P('tile', 'samp')
- sample_grad: bfloat16 [65536, 1024], P('tile', 'samp')
All inputs are finite; a program needn't handle non-finite values.
Results may differ from a plain program's by a relative error of at most 0.012.
Values may be sent and summed in bfloat16 or wider, within the bound.
No kernel may reach another device: no remote copies, remote signals or barrier semaphores. Data moves between devices by JAX's collectives and lax.ppermute only.
A program may use at most 64 MiB of HBM per device.

v0:
```python
import jax
import jax.numpy as jnp
from jax import lax
from jax.experimental import pallas as pl
from jax.experimental.pallas import tpu as pltpu
from jax.sharding import Mesh, PartitionSpec as P


GROUPS = 2
TILE = ("z", "x", "c")
F32 = jnp.float32
BF16 = jnp.bfloat16
VMEM_GRANT = 60 << 20


def ring(size, shift):
    return [(i, (i + shift) % size) for i in range(size)]


def dot(a, b, ca, cb):
    return lax.dot_general(a, b, (((ca,), (cb,)), ((), ())), preferred_element_type=F32)


def at(values, index, axis=0):
    return lax.dynamic_index_in_dim(values, index, axis, keepdims=False)


def area_gradient(linear, counts):
    rate = 1.0 + jax.nn.softplus(linear)
    return (jax.nn.sigmoid(linear) * (counts.astype(F32)[..., None] / rate - 1.0)).astype(BF16)


def exchange(values, axes):
    return lax.all_to_all(values, axes, split_axis=0, concat_axis=0, tiled=True)


def identity(size):
    return (
        lax.broadcasted_iota(jnp.int32, (size, size), 0)
        == lax.broadcasted_iota(jnp.int32, (size, size), 1)
    ).astype(F32).astype(BF16)


def messages_kernel(place, rows_ref, left_ref, out_ref, rows_out, rows_sc):
    @pl.when(pl.program_id(0) == 0)
    def _():
        rows = rows_ref[...].reshape(256, 1024)
        rows_sc[...] = rows
        rows_out[...] = rows

    part = dot(rows_sc[...], left_ref[...], 1, 0).astype(BF16)
    eye = identity(256)
    for half in range(2):
        block = dot(eye, part[:, half * 256 : half * 256 + 256], 1, 1).astype(BF16)
        block = block.reshape(8, 32, 256)
        out_ref[half * 8 : half * 8 + 8, 0:32, :] = block[:, :, :128]
        out_ref[half * 8 : half * 8 + 8, 32:64, :] = block[:, :, 128:]
    out_ref[:, 64:72, :] = jnp.full((16, 8, 128), place[1], jnp.int32).astype(F32).astype(BF16)


def messages(place, area_blocks, left_factors):
    return pl.pallas_call(
        messages_kernel,
        grid_spec=pltpu.PrefetchScalarGridSpec(
            num_scalar_prefetch=1,
            grid=(4,),
            in_specs=[
                pl.BlockSpec((32, None, 8, 1024), lambda i, p: (0, p[0], 0, 0)),
                pl.BlockSpec((1024, 512), lambda i, p: (0, i)),
            ],
            out_specs=[
                pl.BlockSpec((16, 72, 128), lambda i, p: (i, 0, 0)),
                pl.BlockSpec((256, 1024), lambda i, p: (0, 0)),
            ],
            scratch_shapes=[pltpu.VMEM((256, 1024), BF16)],
        ),
        out_shape=[
            jax.ShapeDtypeStruct((64, 72, 128), BF16),
            jax.ShapeDtypeStruct((256, 1024), BF16),
        ],
        compiler_params=pltpu.CompilerParams(vmem_limit_bytes=VMEM_GRANT),
        cost_estimate=pl.CostEstimate(
            flops=2 * 256 * 1024 * 2048, bytes_accessed=6 << 20, transcendentals=0
        ),
        name="messages",
    )(place, area_blocks.reshape(32, 4, 8, 1024), left_factors)


def operator_kernel(place, *refs):
    keep_ref, sources = refs[0], refs[1:14]
    op_refs, eta_refs = refs[14:16], refs[16:18]
    held, lhs, op, sems = refs[18:31], refs[31], refs[32], refs[33]
    copies = [
        pltpu.make_async_copy(source, target, sems.at[n])
        for n, (source, target) in enumerate(zip(sources, held))
    ]
    for copy in copies:
        copy.start()
    came, right, rows = held[:3]
    near, w = held[3:8], held[8:13]
    x, c, y, group = place[0], place[1], place[2], place[3]
    eye = identity(128)
    copies[0].wait()

    @pl.loop(0, 4)
    def _(n):
        lanes = pl.ds(pl.multiple_of(n * 512, 512), 512)
        tiles = pl.ds(n * 16, 16)
        ids = came[tiles, 64:72, :]
        ids = jnp.concatenate([ids] * 4, axis=1).reshape(512, 128)
        ids = dot(eye[:8], ids, 1, 1)[0:1]
        keep = keep_ref[:, lanes]
        for h in range(2):
            part = dot(eye, came[tiles, 32 * h : 32 * h + 32, :].reshape(512, 128), 1, 1)
            for g in range(GROUPS):
                mask = keep * (ids == g).astype(F32)
                lhs[g * 256 + h * 128 : g * 256 + h * 128 + 128, lanes] = (
                    jnp.where(mask > 0.5, part, 0.0).astype(BF16)
                )

    for copy in copies[1:8]:
        copy.wait()
    hot = [jnp.where(group == g, 1.0, 0.0) for g in range(GROUPS)]
    starts = [
        pl.multiple_of(lax.rem(y - s + 4, 4) * 256 + f, 128)
        for s, f in ((0, 0), (1, 0), (2, 0), (2, 128), (3, 0))
    ]

    @pl.loop(0, 4)
    def _(n):
        cells = pl.ds(pl.multiple_of(n * 256, 256), 256)
        extra = jnp.zeros((256, 256), F32)
        for piece, first in zip(near, starts):
            extra += dot(rows[:, pl.ds(first, piece.shape[0])], piece[:, cells], 1, 0)
        block = dot(lhs[...], right[cells, :], 1, 1)
        for g in range(GROUPS):
            span = slice(g * 256, g * 256 + 256)
            op[span, cells] = block[span] + hot[g] * extra

    for dc in range(2):
        for dx in range(4):
            owner = lax.rem(x - dx + 4, 4) * 2 + lax.rem(c + dc, 2)
            pieces = [
                op[pl.ds(pl.multiple_of((low * 8 + owner) * 8 + g * 256, 8), 8), :]
                for g in range(GROUPS)
                for low in range(4)
            ]
            op_refs[dc][dx * 64 : dx * 64 + 64, :] = jnp.concatenate(pieces, axis=0).astype(BF16)
    for copy in copies[8:]:
        copy.wait()
    for dc in range(2):
        for s, piece in ((0, w[0]), (1, w[1]), (3, w[4])):
            eta_refs[dc][:, s * 256 : s * 256 + 256] = dot(
                op_refs[dc][...], piece[...], 1, 0
            ).astype(BF16)
        eta_refs[dc][:, 512:768] = (
            dot(op_refs[dc][:, :512], w[2][...], 1, 0) + dot(op_refs[dc][:, 512:], w[3][...], 1, 0)
        ).astype(BF16)


def operator(place, came, right_factors, rows, near, w, keep):
    sources = (came, right_factors, rows, *near, *w)
    return pl.pallas_call(
        operator_kernel,
        grid_spec=pltpu.PrefetchScalarGridSpec(
            num_scalar_prefetch=1,
            grid=(),
            in_specs=[pl.BlockSpec(memory_space=pltpu.VMEM)]
            + [pl.BlockSpec(memory_space=pl.ANY)] * len(sources),
            out_specs=[pl.BlockSpec(memory_space=pltpu.VMEM)] * 4,
            scratch_shapes=[pltpu.VMEM(v.shape, v.dtype) for v in sources]
            + [
                pltpu.VMEM((512, 2048), BF16),
                pltpu.VMEM((512, 1024), F32),
                pltpu.SemaphoreType.DMA((len(sources),)),
            ],
        ),
        out_shape=[jax.ShapeDtypeStruct((256, 1024), BF16)] * 4,
        compiler_params=pltpu.CompilerParams(vmem_limit_bytes=VMEM_GRANT),
        cost_estimate=pl.CostEstimate(
            flops=2 * 512 * 1024 * 3072, bytes_accessed=11 << 20, transcendentals=0
        ),
        name="operator",
    )(place, keep, *sources)


def gather_y(block):
    half = block.shape[0] // 2
    before = lax.ppermute(block, "y", ring(4, 1))
    after = lax.ppermute(block, "y", ring(4, -1))
    far_top = lax.ppermute(before[:half], "y", ring(4, 1))
    far_low = lax.ppermute(after[half:], "y", ring(4, -1))
    return block, before, far_top, far_low, after


def step(
    samples_w, dense_tiles, left_factors, right_factors, ranks, area_blocks, area_group, counts
):
    z, x, c, y = (lax.axis_index(a) for a in ("z", "x", "c", "y"))
    k = (z * 4 + x) * 2 + c
    group = area_group[0]
    w = gather_y(samples_w)
    sent, rows = messages(jnp.stack([y, group]), area_blocks, left_factors)
    came = exchange(sent, TILE)
    near = gather_y(dense_tiles)
    keep = (jnp.arange(32, dtype=jnp.int32)[None, :] < ranks).astype(F32).reshape(1, 2048)
    top, low, eta_keep, eta_send = operator(
        jnp.stack([x, c, y, group]), came, right_factors, rows, near, w, keep
    )
    eta_came = lax.ppermute(eta_send, "c", ring(2, 1))
    top_before = lax.ppermute(top, "y", ring(4, 1))
    low_after = lax.ppermute(low, "y", ring(4, -1))
    low_before = lax.ppermute(low, "y", ring(4, 1))
    top_after = lax.ppermute(top, "y", ring(4, -1))
    top_far = lax.ppermute(top_before, "y", ring(4, 1))
    low_far = lax.ppermute(low_after, "y", ring(4, -1))
    core_sum = (eta_keep.astype(F32) + eta_came.astype(F32)).astype(BF16).reshape(4, 64, 1024)
    x_sum = core_sum[0].astype(F32)
    came_x = [lax.ppermute(core_sum[s], "x", ring(4, -s)) for s in (2, 1, 3)]
    for part in came_x:
        x_sum = x_sum + part.astype(F32)
    z_parts = exchange(x_sum.astype(BF16).reshape(8, 8, 1024), ("z",))
    linear = jnp.sum(z_parts.astype(F32), axis=0)
    grad = area_gradient(linear, counts.reshape(64, 4, 8)[k, y])

    pieces = grad.reshape(8, 4, 256)
    by_y = jnp.stack([at(pieces, (y - t) % 4, 1) for t in range(4)])
    got = exchange(
        jnp.broadcast_to(by_y[None], (8, 4, 8, 256)).reshape(32, 8, 256), ("z", "y")
    )
    got = got.reshape(8, 4, 8, 256)
    grad_out = at(got, z).reshape(32, 256)
    g_own = jnp.stack([at(got, (y - s) % 4, 1) for s in range(4)])
    by_x = {s: lax.ppermute(g_own, "x", ring(4, s)) for s in (2, 1, 3)}
    row = jnp.stack([g_own, by_x[1], by_x[2], by_x[3]], axis=1).reshape(1024, 256)
    other = lax.ppermute(row, "c", ring(2, 1))
    top_all = jnp.concatenate([top, top_before, top_far, top_after], axis=0)
    low_all = jnp.concatenate([low, low_before, low_far, low_after], axis=0)
    own_part = lax.optimization_barrier(dot(top_all, row, 0, 0))
    return grad_out, (own_part + dot(low_all, other, 0, 0)).astype(BF16)


def solution(mesh):
    plane = Mesh(mesh.devices.reshape(8, 4, 2, 4), ("z", "x", "c", "y"))
    return jax.shard_map(
        step,
        mesh=plane,
        in_specs=(
            P(TILE, "y"),
            P(("z", "x", "c", "y"), None),
            P(TILE, None),
            P(TILE, None),
            P(None, TILE),
            P(TILE, None),
            P(TILE),
            P(),
        ),
        out_specs=(P(TILE, "y"), P(TILE, "y")),
        check_vma=False,
    )
```

profile of v0, /device:TPU:24, one launch (start us, length us, event | category | flops | bytes accessed | tf_op | source)
XLA Modules:
  0.0 139.4 jit_solution(17852500578638190610)
XLA Ops:
  1.3 0.6 pad_add_fusion.1.place
  1.9 6.3 %messages.1 = (bf16[64,72,128]{2,1,0:T(8,128)(2,1)}, bf16[256,1024]{1,0:T(8,128)(2,1)}) custom-call(s32[2]{0:T(128)} %pad_add_fusion.1.place, bf16[32,4,8,1024]{3,2,1,0:T(8,128)(2,1)} %bitcast.44, bf16[1024,2048]{1,0:T(8,128)(2,1)} %left_ref.1), custom_call_target="tpu_custom_call" | custom-call | flops 1073741824 | bytes 6291456 | tf_op jit(solution)/shard_map/messages/pallas_call | solution.py:62
  8.2 11.9 %all-to-all-start = ((bf16[64,72,128]{2,1,0:T(8,128)(2,1)}), bf16[64,72,128]{2,1,0:T(8,128)(2,1)S(1)}, u32[]{:S(2)}, u32[]{:S(2)}) async-start(bf16[64,72,128]{2,1,0:T(8,128)(2,1)} %get-tuple-element.8), calls=%async_computation | async-start | bytes 2359296 | tf_op jit(solution)/shard_map/all_to_all | solution.py:34
  20.1 0.3 collective-permute-start
  20.4 1.8 %collective-permute-start.2 = (bf16[256,1024]{1,0:T(8,128)(2,1)S(1)}, bf16[256,1024]{1,0:T(8,128)(2,1)S(1)}, u32[]{:S(2)}, u32[]{:S(2)}) collective-permute-start(bf16[256,1024]{1,0:T(8,128)(2,1)S(1)} %copy-done.5), channel_id=1, source_target_pairs={{0,3},{1,0},{2,1},{3,2},{4,7},{5,4},{6,5},{7,6},{8,11},{9,8},{10,9... | collective-permute-start | bytes 1572872 | tf_op jit(solution)/shard_map/ppermute | solution.py:190
  22.2 1.4 %collective-permute-start.4 = (bf16[1024,256]{1,0:T(8,128)(2,1)S(1)}, bf16[1024,256]{1,0:T(8,128)(2,1)}, u32[]{:S(2)}, u32[]{:S(2)}) collective-permute-start(bf16[1024,256]{1,0:T(8,128)(2,1)S(1)} %copy-done.6), channel_id=1, source_target_pairs={{0,1},{1,2},{2,3},{3,0},{4,5},{5,6},{6,7},{7,4},{8,9},{9,10},{10,1... | collective-permute-start | bytes 1572872 | tf_op jit(solution)/shard_map/ppermute | solution.py:189
  23.7 0.6 collective-permute-start.6
  24.3 10.7 %collective-permute-done.refs_5_ = bf16[256,1024]{1,0:T(8,128)(2,1)S(1)} collective-permute-done((bf16[256,1024]{1,0:T(8,128)(2,1)S(1)}, bf16[256,1024]{1,0:T(8,128)(2,1)S(1)}, u32[]{:S(2)}, u32[]{:S(2)}) %collective-permute-start) | collective-permute-done | bytes 524320 | tf_op jit(solution)/shard_map/ppermute | solution.py:189
  35.0 1.5 %collective-permute-start.1 = (bf16[128,1024]{1,0:T(8,128)(2,1)S(1)}, bf16[128,1024]{1,0:T(8,128)(2,1)}, u32[]{:S(2)}, u32[]{:S(2)}) collective-permute-start(bf16[128,1024]{1,0:T(8,128)(2,1)S(1)} %slice.36), channel_id=1, source_target_pairs={{0,1},{1,2},{2,3},{3,0},{4,5},{5,6},{6,7},{7,4},{8,9},{9,10},{10,1... | collective-permute-start | bytes 786440 | tf_op jit(solution)/shard_map/ppermute | solution.py:191
  36.6 0.0 collective-permute-done.2.refs_8_
  36.6 0.7 collective-permute-start.3
  37.2 9.1 %collective-permute-done.4.refs_10_ = bf16[1024,256]{1,0:T(8,128)(2,1)} collective-permute-done((bf16[1024,256]{1,0:T(8,128)(2,1)S(1)}, bf16[1024,256]{1,0:T(8,128)(2,1)}, u32[]{:S(2)}, u32[]{:S(2)}) %collective-permute-start.4) | collective-permute-done | bytes 524320 | tf_op jit(solution)/shard_map/ppermute | solution.py:189
  46.3 1.0 slice.38
  47.3 1.5 %collective-permute-start.5 = (bf16[512,256]{1,0:T(8,128)(2,1)S(1)}, bf16[512,256]{1,0:T(8,128)(2,1)}, u32[]{:S(2)}, u32[]{:S(2)}) collective-permute-start(bf16[512,256]{1,0:T(8,128)(2,1)S(1)} %slice.38), channel_id=1, source_target_pairs={{0,1},{1,2},{2,3},{3,0},{4,5},{5,6},{6,7},{7,4},{8,9},{9,10},{10,1... | collective-permute-start | bytes 786440 | tf_op jit(solution)/shard_map/ppermute | solution.py:191
  48.8 0.0 collective-permute-done.6.refs_13_
  48.8 1.0 slice.39
  49.8 0.7 collective-permute-start.7
  50.5 0.1 fusion.22
  50.6 0.7 reshape.92.refs_0_
  51.2 0.7 pad_add_fusion.place
  51.9 0.1 collective-permute-done.1.refs_6_
  52.0 0.8 collective-permute-done.3.refs_7_
  52.8 3.9 %collective-permute-done.5.refs_11_ = bf16[512,256]{1,0:T(8,128)(2,1)} collective-permute-done((bf16[512,256]{1,0:T(8,128)(2,1)S(1)}, bf16[512,256]{1,0:T(8,128)(2,1)}, u32[]{:S(2)}, u32[]{:S(2)}) %collective-permute-start.5) | collective-permute-done | bytes 262176 | tf_op jit(solution)/shard_map/ppermute | solution.py:191
  56.7 1.3 collective-permute-done.7.refs_12_
  58.0 0.0 all-to-all-done.refs_1_
  58.0 1.0 copy-done
  59.0 10.6 %operator.1 = (bf16[256,1024]{1,0:T(8,128)(2,1)}, bf16[256,1024]{1,0:T(8,128)(2,1)}, bf16[256,1024]{1,0:T(8,128)(2,1)}, bf16[256,1024]{1,0:T(8,128)(2,1)}) custom-call(s32[4]{0:T(128)} %pad_add_fusion.place, f32[1,2048]{1,0:T(1,128)} %reshape.92.refs_0_, bf16[64,72,128]{2,1,0:T(8,128)(2,1)} %copy-done, bf16[1024,2048]{1,0:T(8,128)(2,1)} %refs_2_.1, ...), custom_call_target="tpu_custom_call" | custom-call | flops 3221225472 | bytes 11534336 | tf_op jit(solution)/shard_map/operator/pallas_call | solution.py:163
  69.7 0.1 collective-permute-start.8
  69.8 2.1 %collective-permute-done.8 = bf16[256,1024]{1,0:T(8,128)(2,1)S(1)} collective-permute-done((bf16[256,1024]{1,0:T(8,128)(2,1)}, bf16[256,1024]{1,0:T(8,128)(2,1)S(1)}, u32[]{:S(2)}, u32[]{:S(2)}) %collective-permute-start.8) | collective-permute-done | bytes 524320 | tf_op jit(solution)/shard_map/ppermute | solution.py:210
  71.9 1.2 add_convert_fusion.1
  73.2 2.9 %collective-permute-start.10 = (bf16[64,1024]{1,0:T(8,128)(2,1)S(1)}, bf16[64,1024]{1,0:T(8,128)(2,1)S(1)}, u32[]{:S(2)}, u32[]{:S(2)}) collective-permute-start(bf16[64,1024]{1,0:T(8,128)(2,1)S(1)} %get-tuple-element.16), channel_id=1, source_target_pairs={{0,24},{8,0},{16,8},{24,16},{1,25},{9,1},{17,9},{25,17},{2,26},{10... | collective-permute-start | bytes 393224 | tf_op jit(solution)/shard_map/ppermute | solution.py:219
  76.1 0.0 collective-permute-start.11
  76.1 2.3 %collective-permute-start.9 = (bf16[64,1024]{1,0:T(8,128)(2,1)S(1)}, bf16[64,1024]{1,0:T(8,128)(2,1)S(1)}, u32[]{:S(2)}, u32[]{:S(2)}) collective-permute-start(bf16[64,1024]{1,0:T(8,128)(2,1)S(1)} %get-tuple-element.14), channel_id=1, source_target_pairs={{0,16},{8,24},{16,0},{24,8},{1,17},{9,25},{17,1},{25,9},{2,18},{10... | collective-permute-start | bytes 393224 | tf_op jit(solution)/shard_map/ppermute | solution.py:219
  78.4 0.7 collective-permute-done.10
  79.1 6.2 %collective-permute-done.11 = bf16[64,1024]{1,0:T(8,128)(2,1)S(1)} collective-permute-done((bf16[64,1024]{1,0:T(8,128)(2,1)S(1)}, bf16[64,1024]{1,0:T(8,128)(2,1)S(1)}, u32[]{:S(2)}, u32[]{:S(2)}) %collective-permute-start.11) | collective-permute-done | bytes 131104 | tf_op jit(solution)/shard_map/ppermute | solution.py:219
  85.4 0.7 fusion.16
  86.1 6.8 %all-to-all-start.1 = ((bf16[8,8,1024]{2,1,0:T(8,128)(2,1)}), bf16[8,8,1024]{2,1,0:T(8,128)(2,1)S(1)}, u32[]{:S(2)}, u32[]{:S(2)}) async-start(bf16[8,8,1024]{2,1,0:T(8,128)(2,1)} %fusion.16), calls=%async_computation.1 | async-start | bytes 262144 | tf_op jit(solution)/shard_map/all_to_all | solution.py:34
  92.9 0.2 reshape.87
  93.1 0.5 collective-permute-start.19
  93.7 2.8 %collective-permute-start.12 = (bf16[256,1024]{1,0:T(8,128)(2,1)}, bf16[256,1024]{1,0:T(8,128)(2,1)S(1)}, u32[]{:S(2)}, u32[]{:S(2)}) collective-permute-start(bf16[256,1024]{1,0:T(8,128)(2,1)} %get-tuple-element.12), channel_id=1, source_target_pairs={{0,1},{1,2},{2,3},{3,0},{4,5},{5,6},{6,7},{7,4},{8,9},{9,10},{10,1... | collective-permute-start | bytes 1572872 | tf_op jit(solution)/shard_map/ppermute | solution.py:211
  96.4 5.5 %all-to-all-done.1 = bf16[8,8,1024]{2,1,0:T(8,128)(2,1)S(1)} async-done(((bf16[8,8,1024]{2,1,0:T(8,128)(2,1)}), bf16[8,8,1024]{2,1,0:T(8,128)(2,1)S(1)}, u32[]{:S(2)}, u32[]{:S(2)}) %all-to-all-start.1) | async-done | bytes 131104 | tf_op jit(solution)/shard_map/all_to_all | solution.py:34
  102.0 0.1 fusion.21
  102.1 0.7 broadcast_in_dim.2
  102.7 4.7 %all-to-all-start.2 = ((bf16[32,8,256]{2,1,0:T(8,128)(2,1)}), bf16[32,8,256]{2,1,0:T(8,128)(2,1)S(1)}, u32[]{:S(2)}, u32[]{:S(2)}) async-start(bf16[32,8,256]{2,1,0:T(8,128)(2,1)} %bitcast.12), calls=%async_computation.2 | async-start | bytes 262144 | tf_op jit(solution)/shard_map/all_to_all | solution.py:34
  107.4 0.9 collective-permute-start.14
  108.4 0.0 collective-permute-done.12
  108.4 2.4 %collective-permute-start.13 = (bf16[256,1024]{1,0:T(8,128)(2,1)S(1)}, bf16[256,1024]{1,0:T(8,128)(2,1)}, u32[]{:S(2)}, u32[]{:S(2)}) collective-permute-start(bf16[256,1024]{1,0:T(8,128)(2,1)S(1)} %collective-permute-done.12), channel_id=1, source_target_pairs={{0,1},{1,2},{2,3},{3,0},{4,5},{5,6},{6,7},{7,4},{8,9},{9,10},{10,1... | collective-permute-start | bytes 1572872 | tf_op jit(solution)/shard_map/ppermute | solution.py:215
  110.8 5.6 %all-to-all-done.2 = bf16[32,8,256]{2,1,0:T(8,128)(2,1)S(1)} async-done(((bf16[32,8,256]{2,1,0:T(8,128)(2,1)}), bf16[32,8,256]{2,1,0:T(8,128)(2,1)S(1)}, u32[]{:S(2)}, u32[]{:S(2)}) %all-to-all-start.2) | async-done | bytes 131104 | tf_op jit(solution)/shard_map/all_to_all | solution.py:34
  116.5 0.1 collective-permute-start.15
  116.5 1.9 %collective-permute-start.16 = (bf16[4,8,8,256]{3,2,1,0:T(8,128)(2,1)S(1)}, bf16[4,8,8,256]{3,2,1,0:T(8,128)(2,1)S(1)}, u32[]{:S(2)}, u32[]{:S(2)}) collective-permute-start(bf16[4,8,8,256]{3,2,1,0:T(8,128)(2,1)S(1)} %get-tuple-element.18), channel_id=1, source_target_pairs={{0,16},{8,24},{16,0},{24,8},{1,17},{9,25},{17,1},{25,9},{2,18},{10... | collective-permute-start | bytes 393224 | tf_op jit(solution)/shard_map/ppermute | solution.py:234
  118.4 0.0 collective-permute-done.19
  118.4 1.3 collective-permute-start.17
  119.8 4.3 %collective-permute-done.15 = bf16[4,8,8,256]{3,2,1,0:T(8,128)(2,1)S(1)} collective-permute-done((bf16[4,8,8,256]{3,2,1,0:T(8,128)(2,1)S(1)}, bf16[4,8,8,256]{3,2,1,0:T(8,128)(2,1)S(1)}, u32[]{:S(2)}, u32[]{:S(2)}) %collective-permute-start.15) | collective-permute-done | bytes 131104 | tf_op jit(solution)/shard_map/ppermute | solution.py:234
  124.1 1.8 %collective-permute-start.18 = (bf16[256,1024]{1,0:T(8,128)(2,1)S(1)}, bf16[256,1024]{1,0:T(8,128)(2,1)}, u32[]{:S(2)}, u32[]{:S(2)}) collective-permute-start(bf16[256,1024]{1,0:T(8,128)(2,1)S(1)} %copy-done.7), channel_id=1, source_target_pairs={{0,1},{1,2},{2,3},{3,0},{4,5},{5,6},{6,7},{7,4},{8,9},{9,10},{10,1... | collective-permute-start | bytes 1572872 | tf_op jit(solution)/shard_map/ppermute | solution.py:213
  125.9 0.0 collective-permute-done.16
  125.9 0.3 collective-permute-start.20
  126.2 0.1 pad_maximum_fusion
  126.2 0.1 collective-permute-start.21
  126.3 0.6 dynamic-slice_bitcast_fusion.4
  126.9 1.8 %fusion = f32[1024,256]{1,0:T(8,128)S(1)} fusion(bf16[1024,256]{1,0:T(8,128)(2,1)S(1)} %bitcast.48, bf16[256,1024]{1,0:T(8,128)(2,1)S(1)} %collective-permute-done.14, bf16[256,1024]{1,0:T(8,128)(2,1)} %collective-permute-done.13, bf16[256,1024]{1,0:T(8,128)(2,1)S(1)} %collective-permute-done.12, bf16[256,1024]{1,0:T(8,128)(2,1)S(1)} %copy-done.8), kind=kOutput, calls=%fused_computation | convolution fusion | flops 545259520 | bytes 3670016 | tf_op jit(solution)/shard_map/dot_general | solution.py:21
  128.7 4.7 %collective-permute-done.18 = bf16[256,1024]{1,0:T(8,128)(2,1)} collective-permute-done((bf16[256,1024]{1,0:T(8,128)(2,1)S(1)}, bf16[256,1024]{1,0:T(8,128)(2,1)}, u32[]{:S(2)}, u32[]{:S(2)}) %collective-permute-start.18) | collective-permute-done | bytes 524320 | tf_op jit(solution)/shard_map/ppermute | solution.py:213
  133.4 3.0 %collective-permute-done.20 = bf16[256,1024]{1,0:T(8,128)(2,1)} collective-permute-done((bf16[256,1024]{1,0:T(8,128)(2,1)S(1)}, bf16[256,1024]{1,0:T(8,128)(2,1)}, u32[]{:S(2)}, u32[]{:S(2)}) %collective-permute-start.20) | collective-permute-done | bytes 524320 | tf_op jit(solution)/shard_map/ppermute | solution.py:216
  136.4 2.1 %fusion.8 = f32[1024,256]{1,0:T(8,128)S(1)} fusion(bf16[1024,256]{1,0:T(8,128)(2,1)} %collective-permute-done.21, bf16[256,1024]{1,0:T(8,128)(2,1)S(1)} %collective-permute-done.19, bf16[256,1024]{1,0:T(8,128)(2,1)} %collective-permute-done.20, bf16[256,1024]{1,0:T(8,128)(2,1)} %collective-permute-done.18, bf16[256,1024]{1,0:T(8,128)(2,1)S(1)} %copy-done.7), kind=kOutput, calls=%fused_computation.8 | convolution fusion | flops 545259520 | bytes 3670016 | tf_op jit(solution)/shard_map/dot_general | solution.py:21
  138.5 0.9 add_convert_fusion
  (31 shorter events, 0.2 us)
Async XLA Ops:
  1.9 18.3 %copy-start.5 = (bf16[256,1024]{1,0:T(8,128)(2,1)S(1)}, bf16[256,1024]{1,0:T(8,128)(2,1)}, u32[]{:S(2)}) copy-start(bf16[256,1024]{1,0:T(8,128)(2,1)} %refs_4_.1) | copy-start | bytes 1572868
  1.9 20.4 %copy-start.6 = (bf16[1024,256]{1,0:T(8,128)(2,1)S(1)}, bf16[1024,256]{1,0:T(8,128)(2,1)}, u32[]{:S(2)}) copy-start(bf16[1024,256]{1,0:T(8,128)(2,1)} %refs_9_.1) | copy-start | bytes 1572868
  1.9 48.6 %copy-start.4 = (s32[64,1]{0,1:T(1,128)S(1)}, s32[64,1]{0,1:T(1,128)}, u32[]{:S(2)}) copy-start(s32[64,1]{0,1:T(1,128)} %param.12) | copy-start | bytes 772
  8.2 49.8 %all-to-all-start = ((bf16[64,72,128]{2,1,0:T(8,128)(2,1)}), bf16[64,72,128]{2,1,0:T(8,128)(2,1)S(1)}, u32[]{:S(2)}, u32[]{:S(2)}) async-start(bf16[64,72,128]{2,1,0:T(8,128)(2,1)} %get-tuple-element.8), calls=%async_computation | async-start | bytes 2359296 | tf_op jit(solution)/shard_map/all_to_all | solution.py:34
  20.1 14.9 %collective-permute-start = (bf16[256,1024]{1,0:T(8,128)(2,1)S(1)}, bf16[256,1024]{1,0:T(8,128)(2,1)S(1)}, u32[]{:S(2)}, u32[]{:S(2)}) collective-permute-start(bf16[256,1024]{1,0:T(8,128)(2,1)S(1)} %copy-done.5), channel_id=1, source_target_pairs={{0,1},{1,2},{2,3},{3,0},{4,5},{5,6},{6,7},{7,4},{8,9},{9,10},{10,1... | collective-permute-start | bytes 1572872 | tf_op jit(solution)/shard_map/ppermute | solution.py:189
  20.4 16.1 %collective-permute-start.2 = (bf16[256,1024]{1,0:T(8,128)(2,1)S(1)}, bf16[256,1024]{1,0:T(8,128)(2,1)S(1)}, u32[]{:S(2)}, u32[]{:S(2)}) collective-permute-start(bf16[256,1024]{1,0:T(8,128)(2,1)S(1)} %copy-done.5), channel_id=1, source_target_pairs={{0,3},{1,0},{2,1},{3,2},{4,7},{5,4},{6,5},{7,6},{8,11},{9,8},{10,9... | collective-permute-start | bytes 1572872 | tf_op jit(solution)/shard_map/ppermute | solution.py:190
  22.2 24.1 %collective-permute-start.4 = (bf16[1024,256]{1,0:T(8,128)(2,1)S(1)}, bf16[1024,256]{1,0:T(8,128)(2,1)}, u32[]{:S(2)}, u32[]{:S(2)}) collective-permute-start(bf16[1024,256]{1,0:T(8,128)(2,1)S(1)} %copy-done.6), channel_id=1, source_target_pairs={{0,1},{1,2},{2,3},{3,0},{4,5},{5,6},{6,7},{7,4},{8,9},{9,10},{10,1... | collective-permute-start | bytes 1572872 | tf_op jit(solution)/shard_map/ppermute | solution.py:189
  23.7 25.2 %collective-permute-start.6 = (bf16[1024,256]{1,0:T(8,128)(2,1)S(1)}, bf16[1024,256]{1,0:T(8,128)(2,1)}, u32[]{:S(2)}, u32[]{:S(2)}) collective-permute-start(bf16[1024,256]{1,0:T(8,128)(2,1)S(1)} %copy-done.6), channel_id=1, source_target_pairs={{0,3},{1,0},{2,1},{3,2},{4,7},{5,4},{6,5},{7,6},{8,11},{9,8},{10,9... | collective-permute-start | bytes 1572872 | tf_op jit(solution)/shard_map/ppermute | solution.py:190
  35.0 23.0 %copy-start.1 = (bf16[256,1024]{1,0:T(8,128)(2,1)}, bf16[256,1024]{1,0:T(8,128)(2,1)S(1)}, u32[]{:S(2)}) copy-start(bf16[256,1024]{1,0:T(8,128)(2,1)S(1)} %collective-permute-done.refs_5_) | copy-start | bytes 1572868
  35.0 16.9 %collective-permute-start.1 = (bf16[128,1024]{1,0:T(8,128)(2,1)S(1)}, bf16[128,1024]{1,0:T(8,128)(2,1)}, u32[]{:S(2)}, u32[]{:S(2)}) collective-permute-start(bf16[128,1024]{1,0:T(8,128)(2,1)S(1)} %slice.36), channel_id=1, source_target_pairs={{0,1},{1,2},{2,3},{3,0},{4,5},{5,6},{6,7},{7,4},{8,9},{9,10},{10,1... | collective-permute-start | bytes 786440 | tf_op jit(solution)/shard_map/ppermute | solution.py:191
  36.6 21.4 %copy-start.2 = (bf16[256,1024]{1,0:T(8,128)(2,1)}, bf16[256,1024]{1,0:T(8,128)(2,1)S(1)}, u32[]{:S(2)}) copy-start(bf16[256,1024]{1,0:T(8,128)(2,1)S(1)} %collective-permute-done.2.refs_8_) | copy-start | bytes 1572868
  36.6 16.2 %collective-permute-start.3 = (bf16[128,1024]{1,0:T(8,128)(2,1)S(1)}, bf16[128,1024]{1,0:T(8,128)(2,1)}, u32[]{:S(2)}, u32[]{:S(2)}) collective-permute-start(bf16[128,1024]{1,0:T(8,128)(2,1)S(1)} %slice.37), channel_id=1, source_target_pairs={{0,3},{1,0},{2,1},{3,2},{4,7},{5,4},{6,5},{7,6},{8,11},{9,8},{10,9... | collective-permute-start | bytes 786440 | tf_op jit(solution)/shard_map/ppermute | solution.py:192
  47.3 9.4 %collective-permute-start.5 = (bf16[512,256]{1,0:T(8,128)(2,1)S(1)}, bf16[512,256]{1,0:T(8,128)(2,1)}, u32[]{:S(2)}, u32[]{:S(2)}) collective-permute-start(bf16[512,256]{1,0:T(8,128)(2,1)S(1)} %slice.38), channel_id=1, source_target_pairs={{0,1},{1,2},{2,3},{3,0},{4,5},{5,6},{6,7},{7,4},{8,9},{9,10},{10,1... | collective-permute-start | bytes 786440 | tf_op jit(solution)/shard_map/ppermute | solution.py:191
  49.8 8.2 %collective-permute-start.7 = (bf16[512,256]{1,0:T(8,128)(2,1)S(1)}, bf16[512,256]{1,0:T(8,128)(2,1)}, u32[]{:S(2)}, u32[]{:S(2)}) collective-permute-start(bf16[512,256]{1,0:T(8,128)(2,1)S(1)} %slice.39), channel_id=1, source_target_pairs={{0,3},{1,0},{2,1},{3,2},{4,7},{5,4},{6,5},{7,6},{8,11},{9,8},{10,9... | collective-permute-start | bytes 786440 | tf_op jit(solution)/shard_map/ppermute | solution.py:192
  58.0 1.0 copy-start
  59.0 33.9 %copy-start.3 = (s32[2048]{0:T(1024)S(1)}, s32[2048]{0:T(1024)}, u32[]{:S(2)}) copy-start(s32[2048]{0:T(1024)} %param.15) | copy-start | bytes 24580
  69.7 37.8 %copy-start.8 = (bf16[256,1024]{1,0:T(8,128)(2,1)S(1)}, bf16[256,1024]{1,0:T(8,128)(2,1)}, u32[]{:S(2)}) copy-start(bf16[256,1024]{1,0:T(8,128)(2,1)} %get-tuple-element.12) | copy-start | bytes 1572868
  69.7 54.5 %copy-start.7 = (bf16[256,1024]{1,0:T(8,128)(2,1)S(1)}, bf16[256,1024]{1,0:T(8,128)(2,1)}, u32[]{:S(2)}) copy-start(bf16[256,1024]{1,0:T(8,128)(2,1)} %get-tuple-element.13) | copy-start | bytes 1572868
  69.7 2.2 %collective-permute-start.8 = (bf16[256,1024]{1,0:T(8,128)(2,1)}, bf16[256,1024]{1,0:T(8,128)(2,1)S(1)}, u32[]{:S(2)}, u32[]{:S(2)}) collective-permute-start(bf16[256,1024]{1,0:T(8,128)(2,1)} %get-tuple-element.11), channel_id=1, source_target_pairs={{0,4},{4,0},{1,5},{5,1},{2,6},{6,2},{3,7},{7,3},{8,12},{12,8},{9,1... | collective-permute-start | bytes 1572872 | tf_op jit(solution)/shard_map/ppermute | solution.py:210
  73.2 6.0 %collective-permute-start.10 = (bf16[64,1024]{1,0:T(8,128)(2,1)S(1)}, bf16[64,1024]{1,0:T(8,128)(2,1)S(1)}, u32[]{:S(2)}, u32[]{:S(2)}) collective-permute-start(bf16[64,1024]{1,0:T(8,128)(2,1)S(1)} %get-tuple-element.16), channel_id=1, source_target_pairs={{0,24},{8,0},{16,8},{24,16},{1,25},{9,1},{17,9},{25,17},{2,26},{10... | collective-permute-start | bytes 393224 | tf_op jit(solution)/shard_map/ppermute | solution.py:219
  76.1 9.3 %collective-permute-start.11 = (bf16[64,1024]{1,0:T(8,128)(2,1)S(1)}, bf16[64,1024]{1,0:T(8,128)(2,1)S(1)}, u32[]{:S(2)}, u32[]{:S(2)}) collective-permute-start(bf16[64,1024]{1,0:T(8,128)(2,1)S(1)} %get-tuple-element.15), channel_id=1, source_target_pairs={{0,8},{8,16},{16,24},{24,0},{1,9},{9,17},{17,25},{25,1},{2,10},{10... | collective-permute-start | bytes 393224 | tf_op jit(solution)/shard_map/ppermute | solution.py:219
  76.1 9.3 %collective-permute-start.9 = (bf16[64,1024]{1,0:T(8,128)(2,1)S(1)}, bf16[64,1024]{1,0:T(8,128)(2,1)S(1)}, u32[]{:S(2)}, u32[]{:S(2)}) collective-permute-start(bf16[64,1024]{1,0:T(8,128)(2,1)S(1)} %get-tuple-element.14), channel_id=1, source_target_pairs={{0,16},{8,24},{16,0},{24,8},{1,17},{9,25},{17,1},{25,9},{2,18},{10... | collective-permute-start | bytes 393224 | tf_op jit(solution)/shard_map/ppermute | solution.py:219
  86.1 15.9 %all-to-all-start.1 = ((bf16[8,8,1024]{2,1,0:T(8,128)(2,1)}), bf16[8,8,1024]{2,1,0:T(8,128)(2,1)S(1)}, u32[]{:S(2)}, u32[]{:S(2)}) async-start(bf16[8,8,1024]{2,1,0:T(8,128)(2,1)} %fusion.16), calls=%async_computation.1 | async-start | bytes 262144 | tf_op jit(solution)/shard_map/all_to_all | solution.py:34
  93.1 25.3 %collective-permute-start.19 = (bf16[256,1024]{1,0:T(8,128)(2,1)}, bf16[256,1024]{1,0:T(8,128)(2,1)S(1)}, u32[]{:S(2)}, u32[]{:S(2)}) collective-permute-start(bf16[256,1024]{1,0:T(8,128)(2,1)} %get-tuple-element.13), channel_id=1, source_target_pairs={{0,3},{1,0},{2,1},{3,2},{4,7},{5,4},{6,5},{7,6},{8,11},{9,8},{10,9... | collective-permute-start | bytes 1572872 | tf_op jit(solution)/shard_map/ppermute | solution.py:212
  93.7 14.7 %collective-permute-start.12 = (bf16[256,1024]{1,0:T(8,128)(2,1)}, bf16[256,1024]{1,0:T(8,128)(2,1)S(1)}, u32[]{:S(2)}, u32[]{:S(2)}) collective-permute-start(bf16[256,1024]{1,0:T(8,128)(2,1)} %get-tuple-element.12), channel_id=1, source_target_pairs={{0,1},{1,2},{2,3},{3,0},{4,5},{5,6},{6,7},{7,4},{8,9},{9,10},{10,1... | collective-permute-start | bytes 1572872 | tf_op jit(solution)/shard_map/ppermute | solution.py:211
  102.7 13.6 %all-to-all-start.2 = ((bf16[32,8,256]{2,1,0:T(8,128)(2,1)}), bf16[32,8,256]{2,1,0:T(8,128)(2,1)S(1)}, u32[]{:S(2)}, u32[]{:S(2)}) async-start(bf16[32,8,256]{2,1,0:T(8,128)(2,1)} %bitcast.12), calls=%async_computation.2 | async-start | bytes 262144 | tf_op jit(solution)/shard_map/all_to_all | solution.py:34
  107.4 19.5 %collective-permute-start.14 = (bf16[256,1024]{1,0:T(8,128)(2,1)S(1)}, bf16[256,1024]{1,0:T(8,128)(2,1)S(1)}, u32[]{:S(2)}, u32[]{:S(2)}) collective-permute-start(bf16[256,1024]{1,0:T(8,128)(2,1)S(1)} %copy-done.8), channel_id=1, source_target_pairs={{0,3},{1,0},{2,1},{3,2},{4,7},{5,4},{6,5},{7,6},{8,11},{9,8},{10,9... | collective-permute-start | bytes 1572872 | tf_op jit(solution)/shard_map/ppermute | solution.py:214
  108.4 18.6 %collective-permute-start.13 = (bf16[256,1024]{1,0:T(8,128)(2,1)S(1)}, bf16[256,1024]{1,0:T(8,128)(2,1)}, u32[]{:S(2)}, u32[]{:S(2)}) collective-permute-start(bf16[256,1024]{1,0:T(8,128)(2,1)S(1)} %collective-permute-done.12), channel_id=1, source_target_pairs={{0,1},{1,2},{2,3},{3,0},{4,5},{5,6},{6,7},{7,4},{8,9},{9,10},{10,1... | collective-permute-start | bytes 1572872 | tf_op jit(solution)/shard_map/ppermute | solution.py:215
  116.5 7.7 %collective-permute-start.15 = (bf16[4,8,8,256]{3,2,1,0:T(8,128)(2,1)S(1)}, bf16[4,8,8,256]{3,2,1,0:T(8,128)(2,1)S(1)}, u32[]{:S(2)}, u32[]{:S(2)}) collective-permute-start(bf16[4,8,8,256]{3,2,1,0:T(8,128)(2,1)S(1)} %get-tuple-element.18), channel_id=1, source_target_pairs={{0,8},{8,16},{16,24},{24,0},{1,9},{9,17},{17,25},{25,1},{2,10},{10... | collective-permute-start | bytes 393224 | tf_op jit(solution)/shard_map/ppermute | solution.py:234
  116.5 9.3 %collective-permute-start.16 = (bf16[4,8,8,256]{3,2,1,0:T(8,128)(2,1)S(1)}, bf16[4,8,8,256]{3,2,1,0:T(8,128)(2,1)S(1)}, u32[]{:S(2)}, u32[]{:S(2)}) collective-permute-start(bf16[4,8,8,256]{3,2,1,0:T(8,128)(2,1)S(1)} %get-tuple-element.18), channel_id=1, source_target_pairs={{0,16},{8,24},{16,0},{24,8},{1,17},{9,25},{17,1},{25,9},{2,18},{10... | collective-permute-start | bytes 393224 | tf_op jit(solution)/shard_map/ppermute | solution.py:234
  118.4 7.7 %collective-permute-start.17 = (bf16[4,8,8,256]{3,2,1,0:T(8,128)(2,1)S(1)}, bf16[4,8,8,256]{3,2,1,0:T(8,128)(2,1)S(1)}, u32[]{:S(2)}, u32[]{:S(2)}) collective-permute-start(bf16[4,8,8,256]{3,2,1,0:T(8,128)(2,1)S(1)} %get-tuple-element.18), channel_id=1, source_target_pairs={{0,24},{8,0},{16,8},{24,16},{1,25},{9,1},{17,9},{25,17},{2,26},{10... | collective-permute-start | bytes 393224 | tf_op jit(solution)/shard_map/ppermute | solution.py:234
  124.1 9.3 %collective-permute-start.18 = (bf16[256,1024]{1,0:T(8,128)(2,1)S(1)}, bf16[256,1024]{1,0:T(8,128)(2,1)}, u32[]{:S(2)}, u32[]{:S(2)}) collective-permute-start(bf16[256,1024]{1,0:T(8,128)(2,1)S(1)} %copy-done.7), channel_id=1, source_target_pairs={{0,1},{1,2},{2,3},{3,0},{4,5},{5,6},{6,7},{7,4},{8,9},{9,10},{10,1... | collective-permute-start | bytes 1572872 | tf_op jit(solution)/shard_map/ppermute | solution.py:213
  125.9 10.5 %collective-permute-start.20 = (bf16[256,1024]{1,0:T(8,128)(2,1)S(1)}, bf16[256,1024]{1,0:T(8,128)(2,1)}, u32[]{:S(2)}, u32[]{:S(2)}) collective-permute-start(bf16[256,1024]{1,0:T(8,128)(2,1)S(1)} %collective-permute-done.19), channel_id=1, source_target_pairs={{0,3},{1,0},{2,1},{3,2},{4,7},{5,4},{6,5},{7,6},{8,11},{9,8},{10,9... | collective-permute-start | bytes 1572872 | tf_op jit(solution)/shard_map/ppermute | solution.py:216
  126.2 10.2 %collective-permute-start.21 = (bf16[1024,256]{1,0:T(8,128)(2,1)S(1)}, bf16[1024,256]{1,0:T(8,128)(2,1)}, u32[]{:S(2)}, u32[]{:S(2)}) collective-permute-start(bf16[1024,256]{1,0:T(8,128)(2,1)S(1)} %bitcast.47), channel_id=1, source_target_pairs={{0,4},{4,0},{1,5},{5,1},{2,6},{6,2},{3,7},{7,3},{8,12},{12,8},{9,1... | collective-permute-start | bytes 1572872 | tf_op jit(solution)/shard_map/ppermute | solution.py:236
where the time goes:
time: 140 us; the launch traced here: 139 us
  waiting for transfers between devices  58.2 us (42%)
  starting transfers between devices  49.3 us (35%)
  Pallas kernels  16.9 us (12%)
  local copies, waits for them, and re-layouts  5.24 us (4%)
  other arithmetic  4.39 us (3%)
  matrix products  3.88 us (3%)
  between operations  1.51 us (1%)
    all_to_all x3, starting transfers between devices, exchange(): return lax.all_to_all(values, axes, split_axis=0, concat_axis=0, tiled=True)  23.4 us
    ppermute x2, waiting for transfers between devices, gather_y(): before = lax.ppermute(block, 'y', ring(4, 1))  19.8 us
    all_to_all x3, waiting for transfers between devices, exchange(): return lax.all_to_all(values, axes, split_axis=0, concat_axis=0, tiled=True)  11.2 us
    pallas_call x1, Pallas kernels, operator(): pl.pallas_call(operator_kernel, grid_spec=pltpu.PrefetchScalarGridSpec(nu...  10.6 us
    ppermute x3, waiting for transfers between devices, step(): came_x = [lax.ppermute(core_sum[s], 'x', ring(4, -s)) for s in (2, 1, 3)]  6.96 us
    pallas_call x1, Pallas kernels, messages(): pl.pallas_call(messages_kernel, grid_spec=pltpu.PrefetchScalarGridSpec(nu...  6.32 us
    ppermute x3, starting transfers between devices, step(): came_x = [lax.ppermute(core_sum[s], 'x', ring(4, -s)) for s in (2, 1, 3)]  5.24 us
    ppermute x1, waiting for transfers between devices, step(): low_before = lax.ppermute(low, 'y', ring(4, 1))  4.67 us
  transfers between devices with their start and end apart: 25, of which 14 were waited for; matrix products, arithmetic and copies ran while one was open for 5% of the time, Pallas kernels for 0%

commit v1 on v0

v1 whole, which is shorter than its diff:
```python
import jax
import jax.numpy as jnp
from jax import lax
from jax.experimental import pallas as pl
from jax.experimental.pallas import tpu as pltpu
from jax.sharding import Mesh, PartitionSpec as P


GROUPS = 2
TILE = ("z", "x", "c")
F32 = jnp.float32
BF16 = jnp.bfloat16
VMEM_GRANT = 60 << 20


def ring(size, shift):
    return [(i, (i + shift) % size) for i in range(size)]


def dot(a, b, ca, cb):
    return lax.dot_general(a, b, (((ca,), (cb,)), ((), ())), preferred_element_type=F32)


def at(values, index, axis=0):
    return lax.dynamic_index_in_dim(values, index, axis, keepdims=False)


def area_gradient(linear, counts):
    rate = 1.0 + jax.nn.softplus(linear)
    return (jax.nn.sigmoid(linear) * (counts.astype(F32)[..., None] / rate - 1.0)).astype(BF16)


def exchange(values, axes):
    return lax.all_to_all(values, axes, split_axis=0, concat_axis=0, tiled=True)


def identity(size):
    return (
        lax.broadcasted_iota(jnp.int32, (size, size), 0)
        == lax.broadcasted_iota(jnp.int32, (size, size), 1)
    ).astype(F32).astype(BF16)


def messages_kernel(place, rows_hbm, left_hbm, out_hbm, rows_out, parts, left, out, sems):
    y = lax.axis_index("y")
    first = pltpu.make_async_copy(rows_hbm.at[:, y], parts, sems.at[0])
    first.start()
    loads = []
    for n in range(4):
        cols = pl.ds(n * 512, 512)
        loads.append(pltpu.make_async_copy(left_hbm.at[:, cols], left.at[n], sems.at[1 + n]))
        loads[n].start()
    first.wait()
    rows_out[...] = parts[...].reshape(256, 1024)
    ids = jnp.full((16, 8, 128), place[0], jnp.int32).astype(F32).astype(BF16)
    eye = identity(256)
    stores = []
    for n in range(4):
        loads[n].wait()
        part = dot(rows_out[...], left[n], 1, 0).astype(BF16)
        for half in range(2):
            block = dot(eye, part[:, half * 256 : half * 256 + 256], 1, 1).astype(BF16)
            block = block.reshape(8, 32, 256)
            tiles = slice(n * 16 + half * 8, n * 16 + half * 8 + 8)
            out[tiles, 0:32, :] = block[:, :, :128]
            out[tiles, 32:64, :] = block[:, :, 128:]
        out[n * 16 : n * 16 + 16, 64:72, :] = ids
        tiles = pl.ds(n * 16, 16)
        stores.append(pltpu.make_async_copy(out.at[tiles], out_hbm.at[tiles], sems.at[5 + n]))
        stores[n].start()
    for store in stores:
        store.wait()


def messages(place, area_blocks, left_factors):
    return pl.pallas_call(
        messages_kernel,
        grid_spec=pltpu.PrefetchScalarGridSpec(
            num_scalar_prefetch=1,
            grid=(),
            in_specs=[pl.BlockSpec(memory_space=pltpu.HBM)] * 2,
            out_specs=[
                pl.BlockSpec(memory_space=pltpu.HBM),
                pl.BlockSpec(memory_space=pltpu.VMEM),
            ],
            scratch_shapes=[
                pltpu.VMEM((32, 8, 1024), BF16),
                pltpu.VMEM((4, 1024, 512), BF16),
                pltpu.VMEM((64, 72, 128), BF16),
                pltpu.SemaphoreType.DMA((9,)),
            ],
        ),
        out_shape=[
            jax.ShapeDtypeStruct((64, 72, 128), BF16),
            jax.ShapeDtypeStruct((256, 1024), BF16),
        ],
        compiler_params=pltpu.CompilerParams(vmem_limit_bytes=VMEM_GRANT),
        cost_estimate=pl.CostEstimate(
            flops=2 * 256 * 1024 * 2048, bytes_accessed=6 << 20, transcendentals=0
        ),
        name="messages",
    )(place, area_blocks.reshape(32, 4, 8, 1024), left_factors)


def in_vmem(kernel, outs, scratch, flops, grant):
    def call(place, *values):
        size = sum(v.size * v.dtype.itemsize for v in values)
        return pl.pallas_call(
            kernel,
            grid_spec=pltpu.PrefetchScalarGridSpec(
                num_scalar_prefetch=1,
                grid=(),
                in_specs=[pl.BlockSpec(memory_space=pltpu.VMEM)] * len(values),
                out_specs=[pl.BlockSpec(memory_space=pltpu.VMEM)] * len(outs),
                scratch_shapes=scratch,
            ),
            out_shape=[jax.ShapeDtypeStruct(*out) for out in outs],
            compiler_params=pltpu.CompilerParams(vmem_limit_bytes=grant << 20),
            cost_estimate=pl.CostEstimate(flops=flops, bytes_accessed=size, transcendentals=0),
        )(place, *values)

    return call


def offsets_matrix(x, c):
    row = lax.broadcasted_iota(jnp.int32, (256, 256), 0)
    dc, dx, low, r = row >> 7, (row >> 5) & 3, (row >> 3) & 3, row & 7
    area = low * 64 + ((x - dx) & 3) * 16 + ((c + dc) & 1) * 8 + r
    return (lax.broadcasted_iota(jnp.int32, (256, 256), 1) == area).astype(F32).astype(BF16)


def near_kernel(group, rows, *refs):
    d, near, turned = refs[:5], refs[5], refs[6]
    x, c, y = (lax.axis_index(a) for a in ("x", "c", "y"))
    turned[...] = dot(offsets_matrix(x, c), rows[...], 1, 0).astype(BF16)
    starts = [
        pl.multiple_of(lax.rem(y - s + 4, 4) * 256 + f, 128)
        for s, f in ((0, 0), (1, 0), (2, 0), (2, 128), (3, 0))
    ]

    @pl.loop(0, 4)
    def _(n):
        cells = pl.ds(pl.multiple_of(n * 256, 256), 256)
        total = jnp.zeros((256, 256), F32)
        for piece, first in zip(d, starts):
            total += dot(turned[:, pl.ds(first, piece.shape[0])], piece[:, cells], 1, 0)
        near[:, cells] = total


def near_terms(group, rows, d):
    call = in_vmem(
        near_kernel,
        [((256, 1024), F32)],
        [pltpu.VMEM((256, 1024), BF16)],
        2 * 256 * 1024 * 1024,
        60,
    )
    return call(group, rows, *d)[0]


def store_rows(outs, block, hot, extra, cols):
    for g in range(GROUPS):
        part = (block[g * 256 : g * 256 + 256] + hot[g] * extra).astype(BF16)
        for dc in range(2):
            for dx in range(4):
                first = dc * 128 + dx * 32
                outs[dc][dx * 64 + g * 32 : dx * 64 + g * 32 + 32, cols] = part[first : first + 32]


def start_copies(pairs, sems):
    copies = [pltpu.make_async_copy(a, b, sems.at[n]) for n, (a, b) in enumerate(pairs)]
    for copy in copies:
        copy.start()
    return copies


def operator_kernel(group, keep_ref, came, *refs):
    sources, m_refs, eta_refs = refs[:7], refs[7:9], refs[9:11]
    held, lhs, op, sems = refs[11:18], refs[18], refs[19], refs[20]
    near, right, w = held[0], held[1], held[2:]
    pairs = [(sources[0], near)]
    for n in range(4):
        rows = pl.ds(n * 256, 256)
        pairs.append((sources[1].at[rows], right.at[rows]))
    pairs += list(zip(sources[2:], w))
    copies = start_copies(pairs, sems)
    turn = offsets_matrix(lax.axis_index("x"), lax.axis_index("c"))
    pick = identity(128)[:8]

    @pl.loop(0, 4)
    def _(n):
        lanes = pl.ds(pl.multiple_of(n * 512, 512), 512)
        tiles = pl.ds(n * 16, 16)
        ids = came[tiles, 64:72, :]
        ids = jnp.concatenate([ids] * 4, axis=1).reshape(512, 128)
        ids = dot(pick, ids, 1, 1)[0:1]
        keep = keep_ref[:, lanes]
        part = dot(turn[:, :128], came[tiles, 0:32, :].reshape(512, 128), 1, 1)
        part += dot(turn[:, 128:], came[tiles, 32:64, :].reshape(512, 128), 1, 1)
        for g in range(GROUPS):
            mask = keep * (ids == g).astype(F32)
            lhs[g * 256 : g * 256 + 256, lanes] = jnp.where(mask > 0.5, part, 0.0).astype(BF16)

    hot = [jnp.where(group[0] == g, 1.0, 0.0) for g in range(GROUPS)]
    copies[0].wait()
    halves = (op.at[:256], op.at[256:])
    for n in range(4):
        copies[1 + n].wait()
        cells = slice(n * 256, n * 256 + 256)
        store_rows(halves, dot(lhs[...], right[cells, :], 1, 1), hot, near[:, cells], cells)
    outs = start_copies(list(zip(halves, m_refs)), sems.at[10:12])
    for copy in copies[5:]:
        copy.wait()
    for s, spans in ((0, (w[0],)), (1, (w[1],)), (3, (w[4],)), (2, (w[2], w[3]))):
        depth = spans[0].shape[0]
        block = dot(op[:, :depth], spans[0][...], 1, 0)
        for m, span in enumerate(spans[1:]):
            block += dot(op[:, (m + 1) * depth : (m + 2) * depth], span[...], 1, 0)
        for dc in range(2):
            eta_refs[dc][:, s * 256 : s * 256 + 256] = block[dc * 256 : dc * 256 + 256].astype(
                BF16
            )
    for copy in outs:
        copy.wait()


def operator(group, came, keep, near, right_factors, w):
    sources = (near, right_factors, *w)
    return pl.pallas_call(
        operator_kernel,
        grid_spec=pltpu.PrefetchScalarGridSpec(
            num_scalar_prefetch=1,
            grid=(),
            in_specs=[pl.BlockSpec(memory_space=pltpu.VMEM)] * 2
            + [pl.BlockSpec(memory_space=pltpu.HBM)] * len(sources),
            out_specs=[pl.BlockSpec(memory_space=pltpu.HBM)] * 2
            + [pl.BlockSpec(memory_space=pltpu.VMEM)] * 2,
            scratch_shapes=[pltpu.VMEM(v.shape, v.dtype) for v in sources]
            + [
                pltpu.VMEM((512, 2048), BF16),
                pltpu.VMEM((512, 1024), BF16),
                pltpu.SemaphoreType.DMA((12,)),
            ],
        ),
        out_shape=[jax.ShapeDtypeStruct((256, 1024), BF16)] * 4,
        compiler_params=pltpu.CompilerParams(vmem_limit_bytes=VMEM_GRANT),
        cost_estimate=pl.CostEstimate(
            flops=2 * 512 * 1024 * 3072, bytes_accessed=11 << 20, transcendentals=0
        ),
        name="operator",
    )(group, keep, came, *sources)


def gather_y(block):
    half = block.shape[0] // 2
    before = lax.ppermute(block, "y", ring(4, 1))
    after = lax.ppermute(block, "y", ring(4, -1))
    far_top = lax.ppermute(before[:half], "y", ring(4, 1))
    far_low = lax.ppermute(after[half:], "y", ring(4, -1))
    return block, before, far_top, far_low, after


def step(
    samples_w, dense_tiles, left_factors, right_factors, ranks, area_blocks, area_group, counts
):
    z, x, c, y = (lax.axis_index(a) for a in ("z", "x", "c", "y"))
    k = (z * 4 + x) * 2 + c
    d = gather_y(dense_tiles)
    sent, rows = messages(area_group, area_blocks, left_factors)
    came = exchange(sent, TILE)
    w = gather_y(samples_w)
    near = near_terms(area_group, rows, d)
    keep = (jnp.arange(32, dtype=jnp.int32)[None, :] < ranks).astype(F32).reshape(1, 2048)
    top, low, eta_keep, eta_send = operator(
        area_group, came, keep, near, right_factors, w
    )
    eta_came = lax.ppermute(eta_send, "c", ring(2, 1))
    top_before = lax.ppermute(top, "y", ring(4, 1))
    low_after = lax.ppermute(low, "y", ring(4, -1))
    top_far = lax.ppermute(top_before, "y", ring(4, 1))
    low_far = lax.ppermute(low_after, "y", ring(4, -1))
    low_before = lax.ppermute(low, "y", ring(4, 1))
    top_after = lax.ppermute(top, "y", ring(4, -1))
    core_sum = (eta_keep.astype(F32) + eta_came.astype(F32)).astype(BF16).reshape(4, 64, 1024)
    x_sum = core_sum[0].astype(F32)
    came_x = [lax.ppermute(core_sum[s], "x", ring(4, -s)) for s in (2, 1, 3)]
    for part in came_x:
        x_sum = x_sum + part.astype(F32)
    z_parts = exchange(x_sum.astype(BF16).reshape(8, 8, 1024), ("z",))
    linear = jnp.sum(z_parts.astype(F32), axis=0)
    grad = area_gradient(linear, counts.reshape(64, 4, 8)[k, y])

    pieces = grad.reshape(8, 4, 256)
    by_y = jnp.stack([at(pieces, (y - t) % 4, 1) for t in range(4)])
    got = exchange(
        jnp.broadcast_to(by_y[None], (8, 4, 8, 256)).reshape(32, 8, 256), ("z", "y")
    )
    got = got.reshape(8, 4, 8, 256)
    grad_out = at(got, z).reshape(32, 256)
    g_own = jnp.stack([at(got, (y - s) % 4, 1) for s in range(4)])
    by_x = {s: lax.ppermute(g_own, "x", ring(4, s)) for s in (2, 1, 3)}
    row = jnp.stack([g_own, by_x[1], by_x[2], by_x[3]], axis=1).reshape(1024, 256)
    other = lax.ppermute(row, "c", ring(2, 1))
    top_all = jnp.concatenate([top, top_before, top_far, top_after], axis=0)
    low_all = jnp.concatenate([low, low_before, low_far, low_after], axis=0)
    own_part = lax.optimization_barrier(dot(top_all, row, 0, 0))
    return grad_out, (own_part + dot(low_all, other, 0, 0)).astype(BF16)


def solution(mesh):
    plane = Mesh(mesh.devices.reshape(8, 4, 2, 4), ("z", "x", "c", "y"))
    return jax.shard_map(
        step,
        mesh=plane,
        in_specs=(
            P(TILE, "y"),
            P(("z", "x", "c", "y"), None),
            P(TILE, None),
            P(TILE, None),
            P(None, TILE),
            P(TILE, None),
            P(TILE),
            P(),
        ),
        out_specs=(P(TILE, "y"), P(TILE, "y")),
        check_vma=False,
    )
```

time: 140 us -> 138 us (0.986)
  waiting for transfers between devices: 58.2 us -> 54.9 us
  Pallas kernels: 16.9 us -> 20.1 us
    pallas_call x0 -> x1, Pallas kernels: none -> 4.29 us  [call(): pl.pallas_call(kernel, grid_spec=pltpu.PrefetchScalarGridSpec(num_scalar_...]
    ppermute x2, waiting for transfers between devices: 3.93 us -> 1.06 us  [gather_y(): far_top = lax.ppermute(before[:half], 'y', ring(4, 1))]
  transfers between devices with their start and end apart: 25 -> 25, of which waited for: 14 -> 13; matrix products, arithmetic and copies ran while one was open for 5% -> 4% of each run, Pallas kernels for 0% -> 3%
where the time goes in v1:
time: 138 us
  waiting for transfers between devices  54.9 us (40%)
  starting transfers between devices  49.5 us (36%)
  Pallas kernels  20.1 us (15%)
  local copies, waits for them, and re-layouts  4.12 us (3%)
  matrix products  3.88 us (3%)
  other arithmetic  3.75 us (3%)
  between operations  1.53 us (1%)
    all_to_all x3, starting transfers between devices, exchange(): return lax.all_to_all(values, axes, split_axis=0, concat_axis=0, tiled=True)  23.4 us
    ppermute x2, waiting for transfers between devices, gather_y(): before = lax.ppermute(block, 'y', ring(4, 1))  19.7 us
    all_to_all x3, waiting for transfers between devices, exchange(): return lax.all_to_all(values, axes, split_axis=0, concat_axis=0, tiled=True)  11.2 us
    pallas_call x1, Pallas kernels, operator(): pl.pallas_call(operator_kernel, grid_spec=pltpu.PrefetchScalarGridSpec(nu...  10.2 us
    ppermute x3, waiting for transfers between devices, step(): came_x = [lax.ppermute(core_sum[s], 'x', ring(4, -s)) for s in (2, 1, 3)]  6.96 us
    pallas_call x1, Pallas kernels, messages(): pl.pallas_call(messages_kernel, grid_spec=pltpu.PrefetchScalarGridSpec(nu...  5.58 us
    ppermute x3, starting transfers between devices, step(): came_x = [lax.ppermute(core_sum[s], 'x', ring(4, -s)) for s in (2, 1, 3)]  5.24 us
    ppermute x1, waiting for transfers between devices, step(): low_before = lax.ppermute(low, 'y', ring(4, 1))  4.67 us
  transfers between devices with their start and end apart: 25, of which 13 were waited for; matrix products, arithmetic and copies ran while one was open for 4% of the time, Pallas kernels for 3%

profile of v1, /device:TPU:24, one launch (start us, length us, event | category | flops | bytes accessed | tf_op | source)
XLA Modules:
  0.0 137.7 jit_solution(12781188990258912812)
XLA Ops:
  1.3 0.0 copy-start.3
  1.3 5.6 %messages.1 = (bf16[64,72,128]{2,1,0:T(8,128)(2,1)}, bf16[256,1024]{1,0:T(8,128)(2,1)}) custom-call(s32[1]{0:T(128)S(6)} %copy.16.place.group, bf16[32,4,8,1024]{3,2,1,0:T(8,128)(2,1)} %bitcast.41, bf16[1024,2048]{1,0:T(8,128)(2,1)} %left_hbm.1), custom_call_target="tpu_custom_call" | custom-call | flops 1073741824 | bytes 6291456 | tf_op jit(solution)/shard_map/messages/pallas_call | solution.py:76
  6.9 11.9 %all-to-all-start = ((bf16[64,72,128]{2,1,0:T(8,128)(2,1)}), bf16[64,72,128]{2,1,0:T(8,128)(2,1)S(1)}, u32[]{:S(2)}, u32[]{:S(2)}) async-start(bf16[64,72,128]{2,1,0:T(8,128)(2,1)} %get-tuple-element.8), calls=%async_computation | async-start | bytes 2359296 | tf_op jit(solution)/shard_map/all_to_all | solution.py:34
  18.9 0.3 collective-permute-start
  19.2 1.8 %collective-permute-start.2 = (bf16[256,1024]{1,0:T(8,128)(2,1)S(1)}, bf16[256,1024]{1,0:T(8,128)(2,1)S(1)}, u32[]{:S(2)}, u32[]{:S(2)}) collective-permute-start(bf16[256,1024]{1,0:T(8,128)(2,1)S(1)} %copy-done.3), channel_id=1, source_target_pairs={{0,3},{1,0},{2,1},{3,2},{4,7},{5,4},{6,5},{7,6},{8,11},{9,8},{10,9... | collective-permute-start | bytes 1572872 | tf_op jit(solution)/shard_map/ppermute | solution.py:257
  21.0 1.4 %collective-permute-start.4 = (bf16[1024,256]{1,0:T(8,128)(2,1)}, bf16[1024,256]{1,0:T(8,128)(2,1)S(1)}, u32[]{:S(2)}, u32[]{:S(2)}) collective-permute-start(bf16[1024,256]{1,0:T(8,128)(2,1)} %refs_2_.1), channel_id=1, source_target_pairs={{0,1},{1,2},{2,3},{3,0},{4,5},{5,6},{6,7},{7,4},{8,9},{9,10},{10,1... | collective-permute-start | bytes 1572872 | tf_op jit(solution)/shard_map/ppermute | solution.py:256
  22.4 0.6 collective-permute-start.6
  23.0 10.7 %collective-permute-done.refs_1_ = bf16[256,1024]{1,0:T(8,128)(2,1)S(1)} collective-permute-done((bf16[256,1024]{1,0:T(8,128)(2,1)S(1)}, bf16[256,1024]{1,0:T(8,128)(2,1)S(1)}, u32[]{:S(2)}, u32[]{:S(2)}) %collective-permute-start) | collective-permute-done | bytes 524320 | tf_op jit(solution)/shard_map/ppermute | solution.py:256
  33.7 1.5 %collective-permute-start.1 = (bf16[128,1024]{1,0:T(8,128)(2,1)S(1)}, bf16[128,1024]{1,0:T(8,128)(2,1)S(1)}, u32[]{:S(2)}, u32[]{:S(2)}) collective-permute-start(bf16[128,1024]{1,0:T(8,128)(2,1)S(1)} %slice.36), channel_id=1, source_target_pairs={{0,1},{1,2},{2,3},{3,0},{4,5},{5,6},{6,7},{7,4},{8,9},{9,10},{10,1... | collective-permute-start | bytes 786440 | tf_op jit(solution)/shard_map/ppermute | solution.py:258
  35.3 0.0 collective-permute-done.2.refs_4_
  35.3 0.7 collective-permute-start.3
  36.0 9.0 %collective-permute-done.4.refs_3_ = bf16[1024,256]{1,0:T(8,128)(2,1)S(1)} collective-permute-done((bf16[1024,256]{1,0:T(8,128)(2,1)}, bf16[1024,256]{1,0:T(8,128)(2,1)S(1)}, u32[]{:S(2)}, u32[]{:S(2)}) %collective-permute-start.4) | collective-permute-done | bytes 524320 | tf_op jit(solution)/shard_map/ppermute | solution.py:256
  45.0 1.5 %collective-permute-start.5 = (bf16[512,256]{1,0:T(8,128)(2,1)S(1)}, bf16[512,256]{1,0:T(8,128)(2,1)}, u32[]{:S(2)}, u32[]{:S(2)}) collective-permute-start(bf16[512,256]{1,0:T(8,128)(2,1)S(1)} %slice.38), channel_id=1, source_target_pairs={{0,1},{1,2},{2,3},{3,0},{4,5},{5,6},{6,7},{7,4},{8,9},{9,10},{10,1... | collective-permute-start | bytes 786440 | tf_op jit(solution)/shard_map/ppermute | solution.py:258
  46.5 0.0 collective-permute-done.6.refs_6_
  46.5 0.9 collective-permute-start.7
  47.4 0.7 fusion.22
  48.1 1.4 %reshape.92.keep_ref = f32[1,2048]{1,0:T(1,128)} reshape(f32[64,32]{1,0:T(8,128)} %fusion.22) | data formatting | bytes 16384 | tf_op jit(solution)/shard_map/convert_element_type | solution.py:273
  49.5 1.1 collective-permute-done.1.refs_2_
  50.6 1.5 %collective-permute-done.3.refs_3_ = bf16[128,1024]{1,0:T(8,128)(2,1)} collective-permute-done((bf16[128,1024]{1,0:T(8,128)(2,1)S(1)}, bf16[128,1024]{1,0:T(8,128)(2,1)}, u32[]{:S(2)}, u32[]{:S(2)}) %collective-permute-start.3) | collective-permute-done | bytes 262176 | tf_op jit(solution)/shard_map/ppermute | solution.py:259
  52.1 4.3 %shard_map.95.refs_0_ = f32[256,1024]{1,0:T(8,128)} custom-call(s32[1]{0:T(128)S(6)} %copy.16.place.group, bf16[256,1024]{1,0:T(8,128)(2,1)} %get-tuple-element.9.rows, bf16[256,1024]{1,0:T(8,128)(2,1)} %refs_0_.1, bf16[256,1024]{1,0:T(8,128)(2,1)} %copy-done.1, bf16[128,1024]{1,0:T(8,128)(2,1)} %copy-done.4, ...), custom_call_target="tpu_custom_call" | custom-call | flops 536870912 | bytes 2621440 | tf_op jit(solution)/shard_map/pallas_call | solution.py:108
  56.4 0.0 collective-permute-done.5.refs_4_
  56.4 0.3 collective-permute-done.7.refs_5_
  56.7 0.0 all-to-all-done.came
  56.7 1.0 copy-done
  57.7 10.2 %operator.1 = (bf16[256,1024]{1,0:T(8,128)(2,1)}, bf16[256,1024]{1,0:T(8,128)(2,1)}, bf16[256,1024]{1,0:T(8,128)(2,1)}, bf16[256,1024]{1,0:T(8,128)(2,1)}) custom-call(s32[1]{0:T(128)S(6)} %copy.16.place.group, f32[1,2048]{1,0:T(1,128)} %reshape.92.keep_ref, bf16[64,72,128]{2,1,0:T(8,128)(2,1)} %copy-done, f32[256,1024]{1,0:T(8,128)} %shard_map.95.refs_0_, ...), custom_call_target="tpu_custom_call" | custom-call | flops 3221225472 | bytes 11534336 | tf_op jit(solution)/shard_map/operator/pallas_call | solution.py:229
  68.0 0.0 copy-start.10
  68.0 0.1 collective-permute-start.8
  68.1 2.1 %collective-permute-done.8 = bf16[256,1024]{1,0:T(8,128)(2,1)S(1)} collective-permute-done((bf16[256,1024]{1,0:T(8,128)(2,1)}, bf16[256,1024]{1,0:T(8,128)(2,1)S(1)}, u32[]{:S(2)}, u32[]{:S(2)}) %collective-permute-start.8) | collective-permute-done | bytes 524320 | tf_op jit(solution)/shard_map/ppermute | solution.py:277
  70.2 1.2 add_convert_fusion.1
  71.5 2.9 %collective-permute-start.10 = (bf16[64,1024]{1,0:T(8,128)(2,1)S(1)}, bf16[64,1024]{1,0:T(8,128)(2,1)S(1)}, u32[]{:S(2)}, u32[]{:S(2)}) collective-permute-start(bf16[64,1024]{1,0:T(8,128)(2,1)S(1)} %get-tuple-element.16), channel_id=1, source_target_pairs={{0,24},{8,0},{16,8},{24,16},{1,25},{9,1},{17,9},{25,17},{2,26},{10... | collective-permute-start | bytes 393224 | tf_op jit(solution)/shard_map/ppermute | solution.py:286
  74.4 0.0 collective-permute-start.11
  74.4 2.3 %collective-permute-start.9 = (bf16[64,1024]{1,0:T(8,128)(2,1)S(1)}, bf16[64,1024]{1,0:T(8,128)(2,1)S(1)}, u32[]{:S(2)}, u32[]{:S(2)}) collective-permute-start(bf16[64,1024]{1,0:T(8,128)(2,1)S(1)} %get-tuple-element.14), channel_id=1, source_target_pairs={{0,16},{8,24},{16,0},{24,8},{1,17},{9,25},{17,1},{25,9},{2,18},{10... | collective-permute-start | bytes 393224 | tf_op jit(solution)/shard_map/ppermute | solution.py:286
  76.7 0.7 collective-permute-done.10
  77.5 6.2 %collective-permute-done.11 = bf16[64,1024]{1,0:T(8,128)(2,1)S(1)} collective-permute-done((bf16[64,1024]{1,0:T(8,128)(2,1)S(1)}, bf16[64,1024]{1,0:T(8,128)(2,1)S(1)}, u32[]{:S(2)}, u32[]{:S(2)}) %collective-permute-start.11) | collective-permute-done | bytes 131104 | tf_op jit(solution)/shard_map/ppermute | solution.py:286
  83.7 0.0 collective-permute-done.9
  83.7 0.7 fusion.16
  84.4 6.8 %all-to-all-start.1 = ((bf16[8,8,1024]{2,1,0:T(8,128)(2,1)}), bf16[8,8,1024]{2,1,0:T(8,128)(2,1)S(1)}, u32[]{:S(2)}, u32[]{:S(2)}) async-start(bf16[8,8,1024]{2,1,0:T(8,128)(2,1)} %fusion.16), calls=%async_computation.1 | async-start | bytes 262144 | tf_op jit(solution)/shard_map/all_to_all | solution.py:34
  91.2 0.2 reshape.87
  91.4 0.5 collective-permute-start.19
  92.0 2.8 %collective-permute-start.12 = (bf16[256,1024]{1,0:T(8,128)(2,1)}, bf16[256,1024]{1,0:T(8,128)(2,1)S(1)}, u32[]{:S(2)}, u32[]{:S(2)}) collective-permute-start(bf16[256,1024]{1,0:T(8,128)(2,1)} %get-tuple-element.12), channel_id=1, source_target_pairs={{0,1},{1,2},{2,3},{3,0},{4,5},{5,6},{6,7},{7,4},{8,9},{9,10},{10,1... | collective-permute-start | bytes 1572872 | tf_op jit(solution)/shard_map/ppermute | solution.py:278
  94.8 5.5 %all-to-all-done.1 = bf16[8,8,1024]{2,1,0:T(8,128)(2,1)S(1)} async-done(((bf16[8,8,1024]{2,1,0:T(8,128)(2,1)}), bf16[8,8,1024]{2,1,0:T(8,128)(2,1)S(1)}, u32[]{:S(2)}, u32[]{:S(2)}) %all-to-all-start.1) | async-done | bytes 131104 | tf_op jit(solution)/shard_map/all_to_all | solution.py:34
  100.3 0.1 fusion.21
  100.4 0.7 broadcast_in_dim.2
  101.1 4.7 %all-to-all-start.2 = ((bf16[32,8,256]{2,1,0:T(8,128)(2,1)}), bf16[32,8,256]{2,1,0:T(8,128)(2,1)S(1)}, u32[]{:S(2)}, u32[]{:S(2)}) async-start(bf16[32,8,256]{2,1,0:T(8,128)(2,1)} %bitcast.9), calls=%async_computation.2 | async-start | bytes 262144 | tf_op jit(solution)/shard_map/all_to_all | solution.py:34
  105.8 0.9 collective-permute-start.14
  106.7 2.4 %collective-permute-start.13 = (bf16[256,1024]{1,0:T(8,128)(2,1)S(1)}, bf16[256,1024]{1,0:T(8,128)(2,1)}, u32[]{:S(2)}, u32[]{:S(2)}) collective-permute-start(bf16[256,1024]{1,0:T(8,128)(2,1)S(1)} %collective-permute-done.12), channel_id=1, source_target_pairs={{0,1},{1,2},{2,3},{3,0},{4,5},{5,6},{6,7},{7,4},{8,9},{9,10},{10,1... | collective-permute-start | bytes 1572872 | tf_op jit(solution)/shard_map/ppermute | solution.py:280
  109.1 5.6 %all-to-all-done.2 = bf16[32,8,256]{2,1,0:T(8,128)(2,1)S(1)} async-done(((bf16[32,8,256]{2,1,0:T(8,128)(2,1)}), bf16[32,8,256]{2,1,0:T(8,128)(2,1)S(1)}, u32[]{:S(2)}, u32[]{:S(2)}) %all-to-all-start.2) | async-done | bytes 131104 | tf_op jit(solution)/shard_map/all_to_all | solution.py:34
  114.8 0.1 collective-permute-start.15
  114.9 1.9 %collective-permute-start.16 = (bf16[4,8,8,256]{3,2,1,0:T(8,128)(2,1)S(1)}, bf16[4,8,8,256]{3,2,1,0:T(8,128)(2,1)S(1)}, u32[]{:S(2)}, u32[]{:S(2)}) collective-permute-start(bf16[4,8,8,256]{3,2,1,0:T(8,128)(2,1)S(1)} %get-tuple-element.18), channel_id=1, source_target_pairs={{0,16},{8,24},{16,0},{24,8},{1,17},{9,25},{17,1},{25,9},{2,18},{10... | collective-permute-start | bytes 393224 | tf_op jit(solution)/shard_map/ppermute | solution.py:301
  116.8 0.0 collective-permute-done.19
  116.8 1.3 collective-permute-start.17
  118.1 4.3 %collective-permute-done.15 = bf16[4,8,8,256]{3,2,1,0:T(8,128)(2,1)S(1)} collective-permute-done((bf16[4,8,8,256]{3,2,1,0:T(8,128)(2,1)S(1)}, bf16[4,8,8,256]{3,2,1,0:T(8,128)(2,1)S(1)}, u32[]{:S(2)}, u32[]{:S(2)}) %collective-permute-start.15) | collective-permute-done | bytes 131104 | tf_op jit(solution)/shard_map/ppermute | solution.py:301
  122.4 1.8 %collective-permute-start.18 = (bf16[256,1024]{1,0:T(8,128)(2,1)S(1)}, bf16[256,1024]{1,0:T(8,128)(2,1)}, u32[]{:S(2)}, u32[]{:S(2)}) collective-permute-start(bf16[256,1024]{1,0:T(8,128)(2,1)S(1)} %copy-done.9), channel_id=1, source_target_pairs={{0,1},{1,2},{2,3},{3,0},{4,5},{5,6},{6,7},{7,4},{8,9},{9,10},{10,1... | collective-permute-start | bytes 1572872 | tf_op jit(solution)/shard_map/ppermute | solution.py:282
  124.2 0.3 collective-permute-start.20
  124.5 0.0 collective-permute-done.17
  124.5 0.1 pad_maximum_fusion
  124.5 0.1 collective-permute-start.21
  124.6 0.6 dynamic-slice_bitcast_fusion.4
  125.3 1.8 %fusion = f32[1024,256]{1,0:T(8,128)S(1)} fusion(bf16[1024,256]{1,0:T(8,128)(2,1)S(1)} %bitcast.45, bf16[256,1024]{1,0:T(8,128)(2,1)S(1)} %collective-permute-done.14, bf16[256,1024]{1,0:T(8,128)(2,1)} %collective-permute-done.13, bf16[256,1024]{1,0:T(8,128)(2,1)S(1)} %collective-permute-done.12, bf16[256,1024]{1,0:T(8,128)(2,1)S(1)} %copy-done.10), kind=kOutput, calls=%fused_computation | convolution fusion | flops 545259520 | bytes 3670016 | tf_op jit(solution)/shard_map/dot_general | solution.py:21
  127.1 4.7 %collective-permute-done.18 = bf16[256,1024]{1,0:T(8,128)(2,1)} collective-permute-done((bf16[256,1024]{1,0:T(8,128)(2,1)S(1)}, bf16[256,1024]{1,0:T(8,128)(2,1)}, u32[]{:S(2)}, u32[]{:S(2)}) %collective-permute-start.18) | collective-permute-done | bytes 524320 | tf_op jit(solution)/shard_map/ppermute | solution.py:282
  131.7 3.0 %collective-permute-done.20 = bf16[256,1024]{1,0:T(8,128)(2,1)} collective-permute-done((bf16[256,1024]{1,0:T(8,128)(2,1)S(1)}, bf16[256,1024]{1,0:T(8,128)(2,1)}, u32[]{:S(2)}, u32[]{:S(2)}) %collective-permute-start.20) | collective-permute-done | bytes 524320 | tf_op jit(solution)/shard_map/ppermute | solution.py:281
  134.7 0.0 collective-permute-done.21
  134.7 2.1 %fusion.8 = f32[1024,256]{1,0:T(8,128)S(1)} fusion(bf16[1024,256]{1,0:T(8,128)(2,1)} %collective-permute-done.21, bf16[256,1024]{1,0:T(8,128)(2,1)S(1)} %collective-permute-done.19, bf16[256,1024]{1,0:T(8,128)(2,1)} %collective-permute-done.20, bf16[256,1024]{1,0:T(8,128)(2,1)} %collective-permute-done.18, bf16[256,1024]{1,0:T(8,128)(2,1)S(1)} %copy-done.9), kind=kOutput, calls=%fused_computation.8 | convolution fusion | flops 545259520 | bytes 3670016 | tf_op jit(solution)/shard_map/dot_general | solution.py:21
  136.8 0.9 add_convert_fusion
  (34 shorter events, 0.2 us)
Async XLA Ops:
  1.3 17.6 %copy-start.3 = (bf16[256,1024]{1,0:T(8,128)(2,1)S(1)}, bf16[256,1024]{1,0:T(8,128)(2,1)}, u32[]{:S(2)}) copy-start(bf16[256,1024]{1,0:T(8,128)(2,1)} %refs_0_.1) | copy-start | bytes 1572868
  1.3 46.1 %copy-start.8 = (s32[64,1]{0,1:T(1,128)S(1)}, s32[64,1]{0,1:T(1,128)}, u32[]{:S(2)}) copy-start(s32[64,1]{0,1:T(1,128)} %param.12) | copy-start | bytes 772
  6.9 49.8 %all-to-all-start = ((bf16[64,72,128]{2,1,0:T(8,128)(2,1)}), bf16[64,72,128]{2,1,0:T(8,128)(2,1)S(1)}, u32[]{:S(2)}, u32[]{:S(2)}) async-start(bf16[64,72,128]{2,1,0:T(8,128)(2,1)} %get-tuple-element.8), calls=%async_computation | async-start | bytes 2359296 | tf_op jit(solution)/shard_map/all_to_all | solution.py:34
  18.9 14.9 %collective-permute-start = (bf16[256,1024]{1,0:T(8,128)(2,1)S(1)}, bf16[256,1024]{1,0:T(8,128)(2,1)S(1)}, u32[]{:S(2)}, u32[]{:S(2)}) collective-permute-start(bf16[256,1024]{1,0:T(8,128)(2,1)S(1)} %copy-done.3), channel_id=1, source_target_pairs={{0,1},{1,2},{2,3},{3,0},{4,5},{5,6},{6,7},{7,4},{8,9},{9,10},{10,1... | collective-permute-start | bytes 1572872 | tf_op jit(solution)/shard_map/ppermute | solution.py:256
  19.2 16.1 %collective-permute-start.2 = (bf16[256,1024]{1,0:T(8,128)(2,1)S(1)}, bf16[256,1024]{1,0:T(8,128)(2,1)S(1)}, u32[]{:S(2)}, u32[]{:S(2)}) collective-permute-start(bf16[256,1024]{1,0:T(8,128)(2,1)S(1)} %copy-done.3), channel_id=1, source_target_pairs={{0,3},{1,0},{2,1},{3,2},{4,7},{5,4},{6,5},{7,6},{8,11},{9,8},{10,9... | collective-permute-start | bytes 1572872 | tf_op jit(solution)/shard_map/ppermute | solution.py:257
  21.0 24.0 %collective-permute-start.4 = (bf16[1024,256]{1,0:T(8,128)(2,1)}, bf16[1024,256]{1,0:T(8,128)(2,1)S(1)}, u32[]{:S(2)}, u32[]{:S(2)}) collective-permute-start(bf16[1024,256]{1,0:T(8,128)(2,1)} %refs_2_.1), channel_id=1, source_target_pairs={{0,1},{1,2},{2,3},{3,0},{4,5},{5,6},{6,7},{7,4},{8,9},{9,10},{10,1... | collective-permute-start | bytes 1572872 | tf_op jit(solution)/shard_map/ppermute | solution.py:256
  22.4 24.1 %collective-permute-start.6 = (bf16[1024,256]{1,0:T(8,128)(2,1)}, bf16[1024,256]{1,0:T(8,128)(2,1)S(1)}, u32[]{:S(2)}, u32[]{:S(2)}) collective-permute-start(bf16[1024,256]{1,0:T(8,128)(2,1)} %refs_2_.1), channel_id=1, source_target_pairs={{0,3},{1,0},{2,1},{3,2},{4,7},{5,4},{6,5},{7,6},{8,11},{9,8},{10,9... | collective-permute-start | bytes 1572872 | tf_op jit(solution)/shard_map/ppermute | solution.py:257
  33.7 18.4 %copy-start.1 = (bf16[256,1024]{1,0:T(8,128)(2,1)}, bf16[256,1024]{1,0:T(8,128)(2,1)S(1)}, u32[]{:S(2)}) copy-start(bf16[256,1024]{1,0:T(8,128)(2,1)S(1)} %collective-permute-done.refs_1_) | copy-start | bytes 1572868
  33.7 16.8 %collective-permute-start.1 = (bf16[128,1024]{1,0:T(8,128)(2,1)S(1)}, bf16[128,1024]{1,0:T(8,128)(2,1)S(1)}, u32[]{:S(2)}, u32[]{:S(2)}) collective-permute-start(bf16[128,1024]{1,0:T(8,128)(2,1)S(1)} %slice.36), channel_id=1, source_target_pairs={{0,1},{1,2},{2,3},{3,0},{4,5},{5,6},{6,7},{7,4},{8,9},{9,10},{10,1... | collective-permute-start | bytes 786440 | tf_op jit(solution)/shard_map/ppermute | solution.py:258
  35.3 16.9 %copy-start.2 = (bf16[256,1024]{1,0:T(8,128)(2,1)}, bf16[256,1024]{1,0:T(8,128)(2,1)S(1)}, u32[]{:S(2)}) copy-start(bf16[256,1024]{1,0:T(8,128)(2,1)S(1)} %collective-permute-done.2.refs_4_) | copy-start | bytes 1572868
  35.3 16.8 %collective-permute-start.3 = (bf16[128,1024]{1,0:T(8,128)(2,1)S(1)}, bf16[128,1024]{1,0:T(8,128)(2,1)}, u32[]{:S(2)}, u32[]{:S(2)}) collective-permute-start(bf16[128,1024]{1,0:T(8,128)(2,1)S(1)} %slice.37), channel_id=1, source_target_pairs={{0,3},{1,0},{2,1},{3,2},{4,7},{5,4},{6,5},{7,6},{8,11},{9,8},{10,9... | collective-permute-start | bytes 786440 | tf_op jit(solution)/shard_map/ppermute | solution.py:259
  45.0 2.4 %copy-start.5 = (bf16[1024,256]{1,0:T(8,128)(2,1)}, bf16[1024,256]{1,0:T(8,128)(2,1)S(1)}, u32[]{:S(2)}) copy-start(bf16[1024,256]{1,0:T(8,128)(2,1)S(1)} %collective-permute-done.4.refs_3_) | copy-start | bytes 1572868
  45.0 11.4 %collective-permute-start.5 = (bf16[512,256]{1,0:T(8,128)(2,1)S(1)}, bf16[512,256]{1,0:T(8,128)(2,1)}, u32[]{:S(2)}, u32[]{:S(2)}) collective-permute-start(bf16[512,256]{1,0:T(8,128)(2,1)S(1)} %slice.38), channel_id=1, source_target_pairs={{0,1},{1,2},{2,3},{3,0},{4,5},{5,6},{6,7},{7,4},{8,9},{9,10},{10,1... | collective-permute-start | bytes 786440 | tf_op jit(solution)/shard_map/ppermute | solution.py:258
  46.5 0.9 copy-start.6
  46.5 10.2 %collective-permute-start.7 = (bf16[512,256]{1,0:T(8,128)(2,1)S(1)}, bf16[512,256]{1,0:T(8,128)(2,1)}, u32[]{:S(2)}, u32[]{:S(2)}) collective-permute-start(bf16[512,256]{1,0:T(8,128)(2,1)S(1)} %slice.39), channel_id=1, source_target_pairs={{0,3},{1,0},{2,1},{3,2},{4,7},{5,4},{6,5},{7,6},{8,11},{9,8},{10,9... | collective-permute-start | bytes 786440 | tf_op jit(solution)/shard_map/ppermute | solution.py:259
  50.6 1.5 %copy-start.4 = (bf16[128,1024]{1,0:T(8,128)(2,1)}, bf16[128,1024]{1,0:T(8,128)(2,1)S(1)}, u32[]{:S(2)}) copy-start(bf16[128,1024]{1,0:T(8,128)(2,1)S(1)} %collective-permute-done.1.refs_2_) | copy-start | bytes 786436
  56.4 34.8 %copy-start.7 = (s32[2048]{0:T(1024)S(1)}, s32[2048]{0:T(1024)}, u32[]{:S(2)}) copy-start(s32[2048]{0:T(1024)} %param.15) | copy-start | bytes 24580
  56.7 1.0 copy-start
  68.0 37.8 %copy-start.10 = (bf16[256,1024]{1,0:T(8,128)(2,1)S(1)}, bf16[256,1024]{1,0:T(8,128)(2,1)}, u32[]{:S(2)}) copy-start(bf16[256,1024]{1,0:T(8,128)(2,1)} %get-tuple-element.12) | copy-start | bytes 1572868
  68.0 54.4 %copy-start.9 = (bf16[256,1024]{1,0:T(8,128)(2,1)S(1)}, bf16[256,1024]{1,0:T(8,128)(2,1)}, u32[]{:S(2)}) copy-start(bf16[256,1024]{1,0:T(8,128)(2,1)} %get-tuple-element.13) | copy-start | bytes 1572868
  68.0 2.2 %collective-permute-start.8 = (bf16[256,1024]{1,0:T(8,128)(2,1)}, bf16[256,1024]{1,0:T(8,128)(2,1)S(1)}, u32[]{:S(2)}, u32[]{:S(2)}) collective-permute-start(bf16[256,1024]{1,0:T(8,128)(2,1)} %get-tuple-element.11), channel_id=1, source_target_pairs={{0,4},{4,0},{1,5},{5,1},{2,6},{6,2},{3,7},{7,3},{8,12},{12,8},{9,1... | collective-permute-start | bytes 1572872 | tf_op jit(solution)/shard_map/ppermute | solution.py:277
  71.5 6.0 %collective-permute-start.10 = (bf16[64,1024]{1,0:T(8,128)(2,1)S(1)}, bf16[64,1024]{1,0:T(8,128)(2,1)S(1)}, u32[]{:S(2)}, u32[]{:S(2)}) collective-permute-start(bf16[64,1024]{1,0:T(8,128)(2,1)S(1)} %get-tuple-element.16), channel_id=1, source_target_pairs={{0,24},{8,0},{16,8},{24,16},{1,25},{9,1},{17,9},{25,17},{2,26},{10... | collective-permute-start | bytes 393224 | tf_op jit(solution)/shard_map/ppermute | solution.py:286
  74.4 9.3 %collective-permute-start.11 = (bf16[64,1024]{1,0:T(8,128)(2,1)S(1)}, bf16[64,1024]{1,0:T(8,128)(2,1)S(1)}, u32[]{:S(2)}, u32[]{:S(2)}) collective-permute-start(bf16[64,1024]{1,0:T(8,128)(2,1)S(1)} %get-tuple-element.15), channel_id=1, source_target_pairs={{0,8},{8,16},{16,24},{24,0},{1,9},{9,17},{17,25},{25,1},{2,10},{10... | collective-permute-start | bytes 393224 | tf_op jit(solution)/shard_map/ppermute | solution.py:286
  74.4 9.3 %collective-permute-start.9 = (bf16[64,1024]{1,0:T(8,128)(2,1)S(1)}, bf16[64,1024]{1,0:T(8,128)(2,1)S(1)}, u32[]{:S(2)}, u32[]{:S(2)}) collective-permute-start(bf16[64,1024]{1,0:T(8,128)(2,1)S(1)} %get-tuple-element.14), channel_id=1, source_target_pairs={{0,16},{8,24},{16,0},{24,8},{1,17},{9,25},{17,1},{25,9},{2,18},{10... | collective-permute-start | bytes 393224 | tf_op jit(solution)/shard_map/ppermute | solution.py:286
  84.4 15.9 %all-to-all-start.1 = ((bf16[8,8,1024]{2,1,0:T(8,128)(2,1)}), bf16[8,8,1024]{2,1,0:T(8,128)(2,1)S(1)}, u32[]{:S(2)}, u32[]{:S(2)}) async-start(bf16[8,8,1024]{2,1,0:T(8,128)(2,1)} %fusion.16), calls=%async_computation.1 | async-start | bytes 262144 | tf_op jit(solution)/shard_map/all_to_all | solution.py:34
  91.4 25.3 %collective-permute-start.19 = (bf16[256,1024]{1,0:T(8,128)(2,1)}, bf16[256,1024]{1,0:T(8,128)(2,1)S(1)}, u32[]{:S(2)}, u32[]{:S(2)}) collective-permute-start(bf16[256,1024]{1,0:T(8,128)(2,1)} %get-tuple-element.13), channel_id=1, source_target_pairs={{0,3},{1,0},{2,1},{3,2},{4,7},{5,4},{6,5},{7,6},{8,11},{9,8},{10,9... | collective-permute-start | bytes 1572872 | tf_op jit(solution)/shard_map/ppermute | solution.py:279
  92.0 14.7 %collective-permute-start.12 = (bf16[256,1024]{1,0:T(8,128)(2,1)}, bf16[256,1024]{1,0:T(8,128)(2,1)S(1)}, u32[]{:S(2)}, u32[]{:S(2)}) collective-permute-start(bf16[256,1024]{1,0:T(8,128)(2,1)} %get-tuple-element.12), channel_id=1, source_target_pairs={{0,1},{1,2},{2,3},{3,0},{4,5},{5,6},{6,7},{7,4},{8,9},{9,10},{10,1... | collective-permute-start | bytes 1572872 | tf_op jit(solution)/shard_map/ppermute | solution.py:278
  101.1 13.7 %all-to-all-start.2 = ((bf16[32,8,256]{2,1,0:T(8,128)(2,1)}), bf16[32,8,256]{2,1,0:T(8,128)(2,1)S(1)}, u32[]{:S(2)}, u32[]{:S(2)}) async-start(bf16[32,8,256]{2,1,0:T(8,128)(2,1)} %bitcast.9), calls=%async_computation.2 | async-start | bytes 262144 | tf_op jit(solution)/shard_map/all_to_all | solution.py:34
  105.8 19.5 %collective-permute-start.14 = (bf16[256,1024]{1,0:T(8,128)(2,1)S(1)}, bf16[256,1024]{1,0:T(8,128)(2,1)S(1)}, u32[]{:S(2)}, u32[]{:S(2)}) collective-permute-start(bf16[256,1024]{1,0:T(8,128)(2,1)S(1)} %copy-done.10), channel_id=1, source_target_pairs={{0,3},{1,0},{2,1},{3,2},{4,7},{5,4},{6,5},{7,6},{8,11},{9,8},{10,9... | collective-permute-start | bytes 1572872 | tf_op jit(solution)/shard_map/ppermute | solution.py:283
  106.7 18.6 %collective-permute-start.13 = (bf16[256,1024]{1,0:T(8,128)(2,1)S(1)}, bf16[256,1024]{1,0:T(8,128)(2,1)}, u32[]{:S(2)}, u32[]{:S(2)}) collective-permute-start(bf16[256,1024]{1,0:T(8,128)(2,1)S(1)} %collective-permute-done.12), channel_id=1, source_target_pairs={{0,1},{1,2},{2,3},{3,0},{4,5},{5,6},{6,7},{7,4},{8,9},{9,10},{10,1... | collective-permute-start | bytes 1572872 | tf_op jit(solution)/shard_map/ppermute | solution.py:280
  114.8 7.7 %collective-permute-start.15 = (bf16[4,8,8,256]{3,2,1,0:T(8,128)(2,1)S(1)}, bf16[4,8,8,256]{3,2,1,0:T(8,128)(2,1)S(1)}, u32[]{:S(2)}, u32[]{:S(2)}) collective-permute-start(bf16[4,8,8,256]{3,2,1,0:T(8,128)(2,1)S(1)} %get-tuple-element.18), channel_id=1, source_target_pairs={{0,8},{8,16},{16,24},{24,0},{1,9},{9,17},{17,25},{25,1},{2,10},{10... | collective-permute-start | bytes 393224 | tf_op jit(solution)/shard_map/ppermute | solution.py:301
  114.9 9.3 %collective-permute-start.16 = (bf16[4,8,8,256]{3,2,1,0:T(8,128)(2,1)S(1)}, bf16[4,8,8,256]{3,2,1,0:T(8,128)(2,1)S(1)}, u32[]{:S(2)}, u32[]{:S(2)}) collective-permute-start(bf16[4,8,8,256]{3,2,1,0:T(8,128)(2,1)S(1)} %get-tuple-element.18), channel_id=1, source_target_pairs={{0,16},{8,24},{16,0},{24,8},{1,17},{9,25},{17,1},{25,9},{2,18},{10... | collective-permute-start | bytes 393224 | tf_op jit(solution)/shard_map/ppermute | solution.py:301
  116.8 7.7 %collective-permute-start.17 = (bf16[4,8,8,256]{3,2,1,0:T(8,128)(2,1)S(1)}, bf16[4,8,8,256]{3,2,1,0:T(8,128)(2,1)S(1)}, u32[]{:S(2)}, u32[]{:S(2)}) collective-permute-start(bf16[4,8,8,256]{3,2,1,0:T(8,128)(2,1)S(1)} %get-tuple-element.18), channel_id=1, source_target_pairs={{0,24},{8,0},{16,8},{24,16},{1,25},{9,1},{17,9},{25,17},{2,26},{10... | collective-permute-start | bytes 393224 | tf_op jit(solution)/shard_map/ppermute | solution.py:301
  122.4 9.3 %collective-permute-start.18 = (bf16[256,1024]{1,0:T(8,128)(2,1)S(1)}, bf16[256,1024]{1,0:T(8,128)(2,1)}, u32[]{:S(2)}, u32[]{:S(2)}) collective-permute-start(bf16[256,1024]{1,0:T(8,128)(2,1)S(1)} %copy-done.9), channel_id=1, source_target_pairs={{0,1},{1,2},{2,3},{3,0},{4,5},{5,6},{6,7},{7,4},{8,9},{9,10},{10,1... | collective-permute-start | bytes 1572872 | tf_op jit(solution)/shard_map/ppermute | solution.py:282
  124.2 10.5 %collective-permute-start.20 = (bf16[256,1024]{1,0:T(8,128)(2,1)S(1)}, bf16[256,1024]{1,0:T(8,128)(2,1)}, u32[]{:S(2)}, u32[]{:S(2)}) collective-permute-start(bf16[256,1024]{1,0:T(8,128)(2,1)S(1)} %collective-permute-done.19), channel_id=1, source_target_pairs={{0,3},{1,0},{2,1},{3,2},{4,7},{5,4},{6,5},{7,6},{8,11},{9,8},{10,9... | collective-permute-start | bytes 1572872 | tf_op jit(solution)/shard_map/ppermute | solution.py:281
  124.5 10.2 %collective-permute-start.21 = (bf16[1024,256]{1,0:T(8,128)(2,1)S(1)}, bf16[1024,256]{1,0:T(8,128)(2,1)}, u32[]{:S(2)}, u32[]{:S(2)}) collective-permute-start(bf16[1024,256]{1,0:T(8,128)(2,1)S(1)} %bitcast.44), channel_id=1, source_target_pairs={{0,4},{4,0},{1,5},{5,1},{2,6},{6,2},{3,7},{7,3},{8,12},{12,8},{9,1... | collective-permute-start | bytes 1572872 | tf_op jit(solution)/shard_map/ppermute | solution.py:303

commit v2 on v1

--- a/solution.py
+++ b/solution.py
@@ -197,9 +197,10 @@
         keep = keep_ref[:, lanes]
         part = dot(turn[:, :128], came[tiles, 0:32, :].reshape(512, 128), 1, 1)
         part += dot(turn[:, 128:], came[tiles, 32:64, :].reshape(512, 128), 1, 1)
+        part = part.astype(BF16)
         for g in range(GROUPS):
-            mask = keep * (ids == g).astype(F32)
-            lhs[g * 256 : g * 256 + 256, lanes] = jnp.where(mask > 0.5, part, 0.0).astype(BF16)
+            mask = (keep * (ids == g).astype(F32)).astype(BF16)
+            lhs[g * 256 : g * 256 + 256, lanes] = part * mask
 
     hot = [jnp.where(group[0] == g, 1.0, 0.0) for g in range(GROUPS)]
     copies[0].wait()
@@ -243,7 +244,7 @@
             ],
         ),
         out_shape=[jax.ShapeDtypeStruct((256, 1024), BF16)] * 4,
-        compiler_params=pltpu.CompilerParams(vmem_limit_bytes=VMEM_GRANT),
+        compiler_params=pltpu.CompilerParams(vmem_limit_bytes=50 << 20),
         cost_estimate=pl.CostEstimate(
             flops=2 * 512 * 1024 * 3072, bytes_accessed=11 << 20, transcendentals=0
         ),
@@ -292,13 +293,11 @@
 
     pieces = grad.reshape(8, 4, 256)
     by_y = jnp.stack([at(pieces, (y - t) % 4, 1) for t in range(4)])
-    got = exchange(
-        jnp.broadcast_to(by_y[None], (8, 4, 8, 256)).reshape(32, 8, 256), ("z", "y")
-    )
-    got = got.reshape(8, 4, 8, 256)
-    grad_out = at(got, z).reshape(32, 256)
-    g_own = jnp.stack([at(got, (y - s) % 4, 1) for s in range(4)])
+    got = exchange(jnp.broadcast_to(by_y[:, None], (4, 8, 8, 256)).reshape(32, 8, 256), ("y", "z"))
+    got = got.reshape(4, 8, 8, 256)
+    g_own = jnp.stack([at(got, (y - s) % 4) for s in range(4)])
     by_x = {s: lax.ppermute(g_own, "x", ring(4, s)) for s in (2, 1, 3)}
+    grad_out = at(got, z, 1).reshape(32, 256)
     row = jnp.stack([g_own, by_x[1], by_x[2], by_x[3]], axis=1).reshape(1024, 256)
     other = lax.ppermute(row, "c", ring(2, 1))
     top_all = jnp.concatenate([top, top_before, top_far, top_after], axis=0)

time: 138 us -> 135 us (0.978)
  other arithmetic: 3.75 us -> 2.1 us
  local copies, waits for them, and re-layouts: 4.12 us -> 2.48 us
    ppermute x2, waiting for transfers between devices: 1.06 us -> 2.66 us  [gather_y(): far_top = lax.ppermute(before[:half], 'y', ring(4, 1))]
  transfers between devices with their start and end apart: 25 -> 25, of which waited for: 13 -> 13; matrix products, arithmetic and copies ran while one was open for 4% -> 3% of each run, Pallas kernels for 3% -> 3%
where the time goes in v2:
time: 135 us; the launch traced here: 134 us
  waiting for transfers between devices  55.7 us (41%)
  starting transfers between devices  49.6 us (37%)
  Pallas kernels  19.2 us (14%)
  matrix products  3.87 us (3%)
  local copies, waits for them, and re-layouts  2.48 us (2%)
  other arithmetic  2.1 us (2%)
  between operations  1.52 us (1%)
    all_to_all x3, starting transfers between devices, exchange(): return lax.all_to_all(values, axes, split_axis=0, concat_axis=0, tiled=True)  23.7 us
    ppermute x2, waiting for transfers between devices, gather_y(): before = lax.ppermute(block, 'y', ring(4, 1))  19.7 us
    all_to_all x3, waiting for transfers between devices, exchange(): return lax.all_to_all(values, axes, split_axis=0, concat_axis=0, tiled=True)  10.7 us
    pallas_call x1, Pallas kernels, operator(): pl.pallas_call(operator_kernel, grid_spec=pltpu.PrefetchScalarGridSpec(nu...  9.34 us
    ppermute x3, waiting for transfers between devices, step(): came_x = [lax.ppermute(core_sum[s], 'x', ring(4, -s)) for s in (2, 1, 3)]  6.96 us
    pallas_call x1, Pallas kernels, messages(): pl.pallas_call(messages_kernel, grid_spec=pltpu.PrefetchScalarGridSpec(nu...  5.62 us
    ppermute x3, starting transfers between devices, step(): came_x = [lax.ppermute(core_sum[s], 'x', ring(4, -s)) for s in (2, 1, 3)]  5.24 us
    ppermute x1, waiting for transfers between devices, step(): low_before = lax.ppermute(low, 'y', ring(4, 1))  4.62 us
  transfers between devices with their start and end apart: 25, of which 13 were waited for; matrix products, arithmetic and copies ran while one was open for 3% of the time, Pallas kernels for 3%

profile of v2, /device:TPU:24, one launch (start us, length us, event | category | flops | bytes accessed | tf_op | source)
XLA Modules:
  0.0 134.4 jit_solution(11741482997813155025)
XLA Ops:
  1.3 0.0 copy-start.3
  1.3 5.6 %messages.1 = (bf16[64,72,128]{2,1,0:T(8,128)(2,1)}, bf16[256,1024]{1,0:T(8,128)(2,1)}) custom-call(s32[1]{0:T(128)S(6)} %copy.11.place.group, bf16[32,4,8,1024]{3,2,1,0:T(8,128)(2,1)} %bitcast.27, bf16[1024,2048]{1,0:T(8,128)(2,1)} %left_hbm.1), custom_call_target="tpu_custom_call" | custom-call | flops 1073741824 | bytes 6291456 | tf_op jit(solution)/shard_map/messages/pallas_call | solution.py:76
  6.9 12.2 %all-to-all-start = ((bf16[64,72,128]{2,1,0:T(8,128)(2,1)}), bf16[64,72,128]{2,1,0:T(8,128)(2,1)}, u32[]{:S(2)}, u32[]{:S(2)}) async-start(bf16[64,72,128]{2,1,0:T(8,128)(2,1)} %get-tuple-element.8), calls=%async_computation | async-start | bytes 2359296 | tf_op jit(solution)/shard_map/all_to_all | solution.py:34
  19.1 0.3 collective-permute-start
  19.4 1.8 %collective-permute-start.2 = (bf16[256,1024]{1,0:T(8,128)(2,1)S(1)}, bf16[256,1024]{1,0:T(8,128)(2,1)S(1)}, u32[]{:S(2)}, u32[]{:S(2)}) collective-permute-start(bf16[256,1024]{1,0:T(8,128)(2,1)S(1)} %copy-done.3), channel_id=1, source_target_pairs={{0,3},{1,0},{2,1},{3,2},{4,7},{5,4},{6,5},{7,6},{8,11},{9,8},{10,9... | collective-permute-start | bytes 1572872 | tf_op jit(solution)/shard_map/ppermute | solution.py:258
  21.2 1.4 %collective-permute-start.4 = (bf16[1024,256]{1,0:T(8,128)(2,1)S(1)}, bf16[1024,256]{1,0:T(8,128)(2,1)S(1)}, u32[]{:S(2)}, u32[]{:S(2)}) collective-permute-start(bf16[1024,256]{1,0:T(8,128)(2,1)S(1)} %copy-done), channel_id=1, source_target_pairs={{0,1},{1,2},{2,3},{3,0},{4,5},{5,6},{6,7},{7,4},{8,9},{9,10},{10,1... | collective-permute-start | bytes 1572872 | tf_op jit(solution)/shard_map/ppermute | solution.py:257
  22.7 0.6 collective-permute-start.6
  23.3 10.7 %collective-permute-done.refs_1_ = bf16[256,1024]{1,0:T(8,128)(2,1)S(1)} collective-permute-done((bf16[256,1024]{1,0:T(8,128)(2,1)S(1)}, bf16[256,1024]{1,0:T(8,128)(2,1)S(1)}, u32[]{:S(2)}, u32[]{:S(2)}) %collective-permute-start) | collective-permute-done | bytes 524320 | tf_op jit(solution)/shard_map/ppermute | solution.py:257
  34.0 1.5 %collective-permute-start.1 = (bf16[128,1024]{1,0:T(8,128)(2,1)S(1)}, bf16[128,1024]{1,0:T(8,128)(2,1)}, u32[]{:S(2)}, u32[]{:S(2)}) collective-permute-start(bf16[128,1024]{1,0:T(8,128)(2,1)S(1)} %slice.36), channel_id=1, source_target_pairs={{0,1},{1,2},{2,3},{3,0},{4,5},{5,6},{6,7},{7,4},{8,9},{9,10},{10,1... | collective-permute-start | bytes 786440 | tf_op jit(solution)/shard_map/ppermute | solution.py:259
  35.5 0.0 collective-permute-done.2.refs_4_
  35.6 0.7 collective-permute-start.3
  36.2 9.0 %collective-permute-done.4.refs_3_ = bf16[1024,256]{1,0:T(8,128)(2,1)S(1)} collective-permute-done((bf16[1024,256]{1,0:T(8,128)(2,1)S(1)}, bf16[1024,256]{1,0:T(8,128)(2,1)S(1)}, u32[]{:S(2)}, u32[]{:S(2)}) %collective-permute-start.4) | collective-permute-done | bytes 524320 | tf_op jit(solution)/shard_map/ppermute | solution.py:257
  45.3 1.5 %collective-permute-start.5 = (bf16[512,256]{1,0:T(8,128)(2,1)S(1)}, bf16[512,256]{1,0:T(8,128)(2,1)S(1)}, u32[]{:S(2)}, u32[]{:S(2)}) collective-permute-start(bf16[512,256]{1,0:T(8,128)(2,1)S(1)} %slice.38), channel_id=1, source_target_pairs={{0,1},{1,2},{2,3},{3,0},{4,5},{5,6},{6,7},{7,4},{8,9},{9,10},{10,1... | collective-permute-start | bytes 786440 | tf_op jit(solution)/shard_map/ppermute | solution.py:259
  46.8 0.0 collective-permute-done.6.refs_6_
  46.8 0.8 slice.39
  47.5 0.6 collective-permute-start.7
  48.1 0.1 fusion.22
  48.2 0.1 reshape.88.keep_ref
  48.3 2.7 %collective-permute-done.1.refs_2_ = bf16[128,1024]{1,0:T(8,128)(2,1)} collective-permute-done((bf16[128,1024]{1,0:T(8,128)(2,1)S(1)}, bf16[128,1024]{1,0:T(8,128)(2,1)}, u32[]{:S(2)}, u32[]{:S(2)}) %collective-permute-start.1) | collective-permute-done | bytes 262176 | tf_op jit(solution)/shard_map/ppermute | solution.py:259
  51.0 1.4 %collective-permute-done.3.refs_3_ = bf16[128,1024]{1,0:T(8,128)(2,1)} collective-permute-done((bf16[128,1024]{1,0:T(8,128)(2,1)S(1)}, bf16[128,1024]{1,0:T(8,128)(2,1)}, u32[]{:S(2)}, u32[]{:S(2)}) %collective-permute-start.3) | collective-permute-done | bytes 262176 | tf_op jit(solution)/shard_map/ppermute | solution.py:260
  52.4 4.3 %shard_map.95.refs_0_ = f32[256,1024]{1,0:T(8,128)} custom-call(s32[1]{0:T(128)S(6)} %copy.11.place.group, bf16[256,1024]{1,0:T(8,128)(2,1)} %get-tuple-element.9.rows, bf16[256,1024]{1,0:T(8,128)(2,1)} %refs_0_.1, bf16[256,1024]{1,0:T(8,128)(2,1)} %copy-done.1, bf16[128,1024]{1,0:T(8,128)(2,1)} %collective-permute-done.1.refs_2_, ...), custom_call_target="tpu_custom_call" | custom-call | flops 536870912 | bytes 2621440 | tf_op jit(solution)/shard_map/pallas_call | solution.py:108
  56.7 0.0 collective-permute-done.5.refs_4_
  56.7 0.1 collective-permute-done.7.refs_5_
  56.8 0.0 all-to-all-done.came
  56.8 9.3 %operator.1 = (bf16[256,1024]{1,0:T(8,128)(2,1)S(1)}, bf16[256,1024]{1,0:T(8,128)(2,1)S(1)}, bf16[256,1024]{1,0:T(8,128)(2,1)S(1)}, bf16[256,1024]{1,0:T(8,128)(2,1)S(1)}) custom-call(s32[1]{0:T(128)S(6)} %copy.11.place.group, f32[1,2048]{1,0:T(1,128)S(1)} %reshape.88.keep_ref, bf16[64,72,128]{2,1,0:T(8,128)(2,1)} %all-to-all-done.came, ...), custom_call_target="tpu_custom_call" | custom-call | flops 3221225472 | bytes 11534336 | tf_op jit(solution)/shard_map/operator/pallas_call | solution.py:230
  66.2 0.1 collective-permute-start.8
  66.3 1.9 %collective-permute-done.8 = bf16[256,1024]{1,0:T(8,128)(2,1)S(1)} collective-permute-done((bf16[256,1024]{1,0:T(8,128)(2,1)S(1)}, bf16[256,1024]{1,0:T(8,128)(2,1)S(1)}, u32[]{:S(2)}, u32[]{:S(2)}) %collective-permute-start.8) | collective-permute-done | bytes 524320 | tf_op jit(solution)/shard_map/ppermute | solution.py:278
  68.2 0.2 add_convert_fusion.1
  68.4 2.9 %collective-permute-start.10 = (bf16[64,1024]{1,0:T(8,128)(2,1)S(1)}, bf16[64,1024]{1,0:T(8,128)(2,1)S(1)}, u32[]{:S(2)}, u32[]{:S(2)}) collective-permute-start(bf16[64,1024]{1,0:T(8,128)(2,1)S(1)} %get-tuple-element.16), channel_id=1, source_target_pairs={{0,24},{8,0},{16,8},{24,16},{1,25},{9,1},{17,9},{25,17},{2,26},{10... | collective-permute-start | bytes 393224 | tf_op jit(solution)/shard_map/ppermute | solution.py:287
  71.3 0.0 collective-permute-start.11
  71.3 2.3 %collective-permute-start.9 = (bf16[64,1024]{1,0:T(8,128)(2,1)S(1)}, bf16[64,1024]{1,0:T(8,128)(2,1)S(1)}, u32[]{:S(2)}, u32[]{:S(2)}) collective-permute-start(bf16[64,1024]{1,0:T(8,128)(2,1)S(1)} %get-tuple-element.14), channel_id=1, source_target_pairs={{0,16},{8,24},{16,0},{24,8},{1,17},{9,25},{17,1},{25,9},{2,18},{10... | collective-permute-start | bytes 393224 | tf_op jit(solution)/shard_map/ppermute | solution.py:287
  73.6 0.7 collective-permute-done.10
  74.4 6.2 %collective-permute-done.11 = bf16[64,1024]{1,0:T(8,128)(2,1)S(1)} collective-permute-done((bf16[64,1024]{1,0:T(8,128)(2,1)S(1)}, bf16[64,1024]{1,0:T(8,128)(2,1)S(1)}, u32[]{:S(2)}, u32[]{:S(2)}) %collective-permute-start.11) | collective-permute-done | bytes 131104 | tf_op jit(solution)/shard_map/ppermute | solution.py:287
  80.6 0.0 collective-permute-done.9
  80.6 0.7 fusion.16
  81.3 6.8 %all-to-all-start.1 = ((bf16[8,8,1024]{2,1,0:T(8,128)(2,1)}), bf16[8,8,1024]{2,1,0:T(8,128)(2,1)S(1)}, u32[]{:S(2)}, u32[]{:S(2)}) async-start(bf16[8,8,1024]{2,1,0:T(8,128)(2,1)} %fusion.16), calls=%async_computation.1 | async-start | bytes 262144 | tf_op jit(solution)/shard_map/all_to_all | solution.py:34
  88.1 0.2 reshape.83
  88.3 0.5 collective-permute-start.19
  88.9 2.8 %collective-permute-start.12 = (bf16[256,1024]{1,0:T(8,128)(2,1)S(1)}, bf16[256,1024]{1,0:T(8,128)(2,1)S(1)}, u32[]{:S(2)}, u32[]{:S(2)}) collective-permute-start(bf16[256,1024]{1,0:T(8,128)(2,1)S(1)} %get-tuple-element.12), channel_id=1, source_target_pairs={{0,1},{1,2},{2,3},{3,0},{4,5},{5,6},{6,7},{7,4},{8,9},{9,10},{10,1... | collective-permute-start | bytes 1572872 | tf_op jit(solution)/shard_map/ppermute | solution.py:279
  91.7 5.5 %all-to-all-done.1 = bf16[8,8,1024]{2,1,0:T(8,128)(2,1)S(1)} async-done(((bf16[8,8,1024]{2,1,0:T(8,128)(2,1)}), bf16[8,8,1024]{2,1,0:T(8,128)(2,1)S(1)}, u32[]{:S(2)}, u32[]{:S(2)}) %all-to-all-start.1) | async-done | bytes 131104 | tf_op jit(solution)/shard_map/all_to_all | solution.py:34
  97.2 0.1 fusion.21
  97.3 0.7 broadcast_in_dim.2
  98.0 4.7 %all-to-all-start.2 = ((bf16[32,8,256]{2,1,0:T(8,128)(2,1)}), bf16[32,8,256]{2,1,0:T(8,128)(2,1)S(1)}, u32[]{:S(2)}, u32[]{:S(2)}) async-start(bf16[32,8,256]{2,1,0:T(8,128)(2,1)} %bitcast.9), calls=%async_computation.2 | async-start | bytes 262144 | tf_op jit(solution)/shard_map/all_to_all | solution.py:34
  102.7 0.9 collective-permute-start.14
  103.6 0.0 collective-permute-done.12
  103.6 2.4 %collective-permute-start.13 = (bf16[256,1024]{1,0:T(8,128)(2,1)S(1)}, bf16[256,1024]{1,0:T(8,128)(2,1)}, u32[]{:S(2)}, u32[]{:S(2)}) collective-permute-start(bf16[256,1024]{1,0:T(8,128)(2,1)S(1)} %collective-permute-done.12), channel_id=1, source_target_pairs={{0,1},{1,2},{2,3},{3,0},{4,5},{5,6},{6,7},{7,4},{8,9},{9,10},{10,1... | collective-permute-start | bytes 1572872 | tf_op jit(solution)/shard_map/ppermute | solution.py:281
  106.0 5.2 %all-to-all-done.2 = bf16[32,8,256]{2,1,0:T(8,128)(2,1)S(1)} async-done(((bf16[32,8,256]{2,1,0:T(8,128)(2,1)}), bf16[32,8,256]{2,1,0:T(8,128)(2,1)S(1)}, u32[]{:S(2)}, u32[]{:S(2)}) %all-to-all-start.2) | async-done | bytes 131104 | tf_op jit(solution)/shard_map/all_to_all | solution.py:34
  111.3 0.1 collective-permute-start.15
  111.4 1.9 %collective-permute-start.16 = (bf16[4,8,8,256]{3,2,1,0:T(8,128)(2,1)S(1)}, bf16[4,8,8,256]{3,2,1,0:T(8,128)(2,1)S(1)}, u32[]{:S(2)}, u32[]{:S(2)}) collective-permute-start(bf16[4,8,8,256]{3,2,1,0:T(8,128)(2,1)S(1)} %get-tuple-element.18), channel_id=1, source_target_pairs={{0,16},{8,24},{16,0},{24,8},{1,17},{9,25},{17,1},{25,9},{2,18},{10... | collective-permute-start | bytes 393224 | tf_op jit(solution)/shard_map/ppermute | solution.py:299
  113.3 1.4 %collective-permute-start.17 = (bf16[4,8,8,256]{3,2,1,0:T(8,128)(2,1)S(1)}, bf16[4,8,8,256]{3,2,1,0:T(8,128)(2,1)S(1)}, u32[]{:S(2)}, u32[]{:S(2)}) collective-permute-start(bf16[4,8,8,256]{3,2,1,0:T(8,128)(2,1)S(1)} %get-tuple-element.18), channel_id=1, source_target_pairs={{0,24},{8,0},{16,8},{24,16},{1,25},{9,1},{17,9},{25,17},{2,26},{10... | collective-permute-start | bytes 393224 | tf_op jit(solution)/shard_map/ppermute | solution.py:299
  114.7 4.3 %collective-permute-done.15 = bf16[4,8,8,256]{3,2,1,0:T(8,128)(2,1)S(1)} collective-permute-done((bf16[4,8,8,256]{3,2,1,0:T(8,128)(2,1)S(1)}, bf16[4,8,8,256]{3,2,1,0:T(8,128)(2,1)S(1)}, u32[]{:S(2)}, u32[]{:S(2)}) %collective-permute-start.15) | collective-permute-done | bytes 131104 | tf_op jit(solution)/shard_map/ppermute | solution.py:299
  118.9 2.0 %collective-permute-start.18 = (bf16[256,1024]{1,0:T(8,128)(2,1)S(1)}, bf16[256,1024]{1,0:T(8,128)(2,1)}, u32[]{:S(2)}, u32[]{:S(2)}) collective-permute-start(bf16[256,1024]{1,0:T(8,128)(2,1)S(1)} %get-tuple-element.13), channel_id=1, source_target_pairs={{0,1},{1,2},{2,3},{3,0},{4,5},{5,6},{6,7},{7,4},{8,9},{9,10},{10,1... | collective-permute-start | bytes 1572872 | tf_op jit(solution)/shard_map/ppermute | solution.py:283
  120.9 0.0 collective-permute-done.16
  120.9 0.0 collective-permute-start.20
  121.0 0.1 pad_maximum_fusion
  121.1 0.1 collective-permute-start.21
  121.2 0.6 dynamic-slice_bitcast_fusion
  121.8 0.0 collective-permute-done.14
  121.8 0.0 collective-permute-done.13
  121.8 1.8 %fusion = f32[1024,256]{1,0:T(8,128)S(1)} fusion(bf16[1024,256]{1,0:T(8,128)(2,1)S(1)} %bitcast.31, bf16[256,1024]{1,0:T(8,128)(2,1)S(1)} %collective-permute-done.14, bf16[256,1024]{1,0:T(8,128)(2,1)} %collective-permute-done.13, bf16[256,1024]{1,0:T(8,128)(2,1)S(1)} %collective-permute-done.12, bf16[256,1024]{1,0:T(8,128)(2,1)S(1)} %get-tuple-element.12), kind=kOutput, calls=%fused_computation | convolution fusion | flops 545259520 | bytes 3670016 | tf_op jit(solution)/shard_map/dot_general | solution.py:21
  123.6 4.6 %collective-permute-done.18 = bf16[256,1024]{1,0:T(8,128)(2,1)} collective-permute-done((bf16[256,1024]{1,0:T(8,128)(2,1)S(1)}, bf16[256,1024]{1,0:T(8,128)(2,1)}, u32[]{:S(2)}, u32[]{:S(2)}) %collective-permute-start.18) | collective-permute-done | bytes 524320 | tf_op jit(solution)/shard_map/ppermute | solution.py:283
  128.2 3.2 %collective-permute-done.20 = bf16[256,1024]{1,0:T(8,128)(2,1)} collective-permute-done((bf16[256,1024]{1,0:T(8,128)(2,1)S(1)}, bf16[256,1024]{1,0:T(8,128)(2,1)}, u32[]{:S(2)}, u32[]{:S(2)}) %collective-permute-start.20) | collective-permute-done | bytes 524320 | tf_op jit(solution)/shard_map/ppermute | solution.py:282
  131.4 2.1 %fusion.8 = f32[1024,256]{1,0:T(8,128)S(1)} fusion(bf16[1024,256]{1,0:T(8,128)(2,1)} %collective-permute-done.21, bf16[256,1024]{1,0:T(8,128)(2,1)S(1)} %collective-permute-done.19, bf16[256,1024]{1,0:T(8,128)(2,1)} %collective-permute-done.20, bf16[256,1024]{1,0:T(8,128)(2,1)} %collective-permute-done.18, bf16[256,1024]{1,0:T(8,128)(2,1)S(1)} %get-tuple-element.13), kind=kOutput, calls=%fused_computation.8 | convolution fusion | flops 545259520 | bytes 3670016 | tf_op jit(solution)/shard_map/dot_general | solution.py:21
  133.5 0.9 add_convert_fusion
  (27 shorter events, 0.2 us)
Async XLA Ops:
  1.3 17.8 %copy-start.3 = (bf16[256,1024]{1,0:T(8,128)(2,1)S(1)}, bf16[256,1024]{1,0:T(8,128)(2,1)}, u32[]{:S(2)}) copy-start(bf16[256,1024]{1,0:T(8,128)(2,1)} %refs_0_.1) | copy-start | bytes 1572868
  1.3 20.0 %copy-start = (bf16[1024,256]{1,0:T(8,128)(2,1)S(1)}, bf16[1024,256]{1,0:T(8,128)(2,1)}, u32[]{:S(2)}) copy-start(bf16[1024,256]{1,0:T(8,128)(2,1)} %refs_2_.1) | copy-start | bytes 1572868
  1.3 46.8 %copy-start.6 = (s32[64,1]{0,1:T(1,128)S(1)}, s32[64,1]{0,1:T(1,128)}, u32[]{:S(2)}) copy-start(s32[64,1]{0,1:T(1,128)} %param.12) | copy-start | bytes 772
  6.9 49.9 %all-to-all-start = ((bf16[64,72,128]{2,1,0:T(8,128)(2,1)}), bf16[64,72,128]{2,1,0:T(8,128)(2,1)}, u32[]{:S(2)}, u32[]{:S(2)}) async-start(bf16[64,72,128]{2,1,0:T(8,128)(2,1)} %get-tuple-element.8), calls=%async_computation | async-start | bytes 2359296 | tf_op jit(solution)/shard_map/all_to_all | solution.py:34
  19.1 14.9 %collective-permute-start = (bf16[256,1024]{1,0:T(8,128)(2,1)S(1)}, bf16[256,1024]{1,0:T(8,128)(2,1)S(1)}, u32[]{:S(2)}, u32[]{:S(2)}) collective-permute-start(bf16[256,1024]{1,0:T(8,128)(2,1)S(1)} %copy-done.3), channel_id=1, source_target_pairs={{0,1},{1,2},{2,3},{3,0},{4,5},{5,6},{6,7},{7,4},{8,9},{9,10},{10,1... | collective-permute-start | bytes 1572872 | tf_op jit(solution)/shard_map/ppermute | solution.py:257
  19.4 16.1 %collective-permute-start.2 = (bf16[256,1024]{1,0:T(8,128)(2,1)S(1)}, bf16[256,1024]{1,0:T(8,128)(2,1)S(1)}, u32[]{:S(2)}, u32[]{:S(2)}) collective-permute-start(bf16[256,1024]{1,0:T(8,128)(2,1)S(1)} %copy-done.3), channel_id=1, source_target_pairs={{0,3},{1,0},{2,1},{3,2},{4,7},{5,4},{6,5},{7,6},{8,11},{9,8},{10,9... | collective-permute-start | bytes 1572872 | tf_op jit(solution)/shard_map/ppermute | solution.py:258
  21.2 24.0 %collective-permute-start.4 = (bf16[1024,256]{1,0:T(8,128)(2,1)S(1)}, bf16[1024,256]{1,0:T(8,128)(2,1)S(1)}, u32[]{:S(2)}, u32[]{:S(2)}) collective-permute-start(bf16[1024,256]{1,0:T(8,128)(2,1)S(1)} %copy-done), channel_id=1, source_target_pairs={{0,1},{1,2},{2,3},{3,0},{4,5},{5,6},{6,7},{7,4},{8,9},{9,10},{10,1... | collective-permute-start | bytes 1572872 | tf_op jit(solution)/shard_map/ppermute | solution.py:257
  22.7 24.1 %collective-permute-start.6 = (bf16[1024,256]{1,0:T(8,128)(2,1)S(1)}, bf16[1024,256]{1,0:T(8,128)(2,1)S(1)}, u32[]{:S(2)}, u32[]{:S(2)}) collective-permute-start(bf16[1024,256]{1,0:T(8,128)(2,1)S(1)} %copy-done), channel_id=1, source_target_pairs={{0,3},{1,0},{2,1},{3,2},{4,7},{5,4},{6,5},{7,6},{8,11},{9,8},{10,9... | collective-permute-start | bytes 1572872 | tf_op jit(solution)/shard_map/ppermute | solution.py:258
  34.0 18.4 %copy-start.1 = (bf16[256,1024]{1,0:T(8,128)(2,1)}, bf16[256,1024]{1,0:T(8,128)(2,1)S(1)}, u32[]{:S(2)}) copy-start(bf16[256,1024]{1,0:T(8,128)(2,1)S(1)} %collective-permute-done.refs_1_) | copy-start | bytes 1572868
  34.0 16.9 %collective-permute-start.1 = (bf16[128,1024]{1,0:T(8,128)(2,1)S(1)}, bf16[128,1024]{1,0:T(8,128)(2,1)}, u32[]{:S(2)}, u32[]{:S(2)}) collective-permute-start(bf16[128,1024]{1,0:T(8,128)(2,1)S(1)} %slice.36), channel_id=1, source_target_pairs={{0,1},{1,2},{2,3},{3,0},{4,5},{5,6},{6,7},{7,4},{8,9},{9,10},{10,1... | collective-permute-start | bytes 786440 | tf_op jit(solution)/shard_map/ppermute | solution.py:259
  35.5 16.9 %copy-start.2 = (bf16[256,1024]{1,0:T(8,128)(2,1)}, bf16[256,1024]{1,0:T(8,128)(2,1)S(1)}, u32[]{:S(2)}) copy-start(bf16[256,1024]{1,0:T(8,128)(2,1)S(1)} %collective-permute-done.2.refs_4_) | copy-start | bytes 1572868
  35.6 16.8 %collective-permute-start.3 = (bf16[128,1024]{1,0:T(8,128)(2,1)S(1)}, bf16[128,1024]{1,0:T(8,128)(2,1)}, u32[]{:S(2)}, u32[]{:S(2)}) collective-permute-start(bf16[128,1024]{1,0:T(8,128)(2,1)S(1)} %slice.37), channel_id=1, source_target_pairs={{0,3},{1,0},{2,1},{3,2},{4,7},{5,4},{6,5},{7,6},{8,11},{9,8},{10,9... | collective-permute-start | bytes 786440 | tf_op jit(solution)/shard_map/ppermute | solution.py:260
  45.3 11.4 %collective-permute-start.5 = (bf16[512,256]{1,0:T(8,128)(2,1)S(1)}, bf16[512,256]{1,0:T(8,128)(2,1)S(1)}, u32[]{:S(2)}, u32[]{:S(2)}) collective-permute-start(bf16[512,256]{1,0:T(8,128)(2,1)S(1)} %slice.38), channel_id=1, source_target_pairs={{0,1},{1,2},{2,3},{3,0},{4,5},{5,6},{6,7},{7,4},{8,9},{9,10},{10,1... | collective-permute-start | bytes 786440 | tf_op jit(solution)/shard_map/ppermute | solution.py:259
  46.8 1.4 %copy-start.4 = (bf16[1024,256]{1,0:T(8,128)(2,1)}, bf16[1024,256]{1,0:T(8,128)(2,1)S(1)}, u32[]{:S(2)}) copy-start(bf16[1024,256]{1,0:T(8,128)(2,1)S(1)} %collective-permute-done.6.refs_6_) | copy-start | bytes 1572868
  47.5 9.3 %collective-permute-start.7 = (bf16[512,256]{1,0:T(8,128)(2,1)}, bf16[512,256]{1,0:T(8,128)(2,1)S(1)}, u32[]{:S(2)}, u32[]{:S(2)}) collective-permute-start(bf16[512,256]{1,0:T(8,128)(2,1)} %slice.39), channel_id=1, source_target_pairs={{0,3},{1,0},{2,1},{3,2},{4,7},{5,4},{6,5},{7,6},{8,11},{9,8},{10,9... | collective-permute-start | bytes 786440 | tf_op jit(solution)/shard_map/ppermute | solution.py:260
  56.7 31.4 %copy-start.5 = (s32[2048]{0:T(1024)S(1)}, s32[2048]{0:T(1024)}, u32[]{:S(2)}) copy-start(s32[2048]{0:T(1024)} %param.15) | copy-start | bytes 24580
  66.2 2.0 %collective-permute-start.8 = (bf16[256,1024]{1,0:T(8,128)(2,1)S(1)}, bf16[256,1024]{1,0:T(8,128)(2,1)S(1)}, u32[]{:S(2)}, u32[]{:S(2)}) collective-permute-start(bf16[256,1024]{1,0:T(8,128)(2,1)S(1)} %get-tuple-element.11), channel_id=1, source_target_pairs={{0,4},{4,0},{1,5},{5,1},{2,6},{6,2},{3,7},{7,3},{8,12},{12,8},{9,1... | collective-permute-start | bytes 1572872 | tf_op jit(solution)/shard_map/ppermute | solution.py:278
  68.4 6.0 %collective-permute-start.10 = (bf16[64,1024]{1,0:T(8,128)(2,1)S(1)}, bf16[64,1024]{1,0:T(8,128)(2,1)S(1)}, u32[]{:S(2)}, u32[]{:S(2)}) collective-permute-start(bf16[64,1024]{1,0:T(8,128)(2,1)S(1)} %get-tuple-element.16), channel_id=1, source_target_pairs={{0,24},{8,0},{16,8},{24,16},{1,25},{9,1},{17,9},{25,17},{2,26},{10... | collective-permute-start | bytes 393224 | tf_op jit(solution)/shard_map/ppermute | solution.py:287
  71.3 9.3 %collective-permute-start.11 = (bf16[64,1024]{1,0:T(8,128)(2,1)S(1)}, bf16[64,1024]{1,0:T(8,128)(2,1)S(1)}, u32[]{:S(2)}, u32[]{:S(2)}) collective-permute-start(bf16[64,1024]{1,0:T(8,128)(2,1)S(1)} %get-tuple-element.15), channel_id=1, source_target_pairs={{0,8},{8,16},{16,24},{24,0},{1,9},{9,17},{17,25},{25,1},{2,10},{10... | collective-permute-start | bytes 393224 | tf_op jit(solution)/shard_map/ppermute | solution.py:287
  71.3 9.3 %collective-permute-start.9 = (bf16[64,1024]{1,0:T(8,128)(2,1)S(1)}, bf16[64,1024]{1,0:T(8,128)(2,1)S(1)}, u32[]{:S(2)}, u32[]{:S(2)}) collective-permute-start(bf16[64,1024]{1,0:T(8,128)(2,1)S(1)} %get-tuple-element.14), channel_id=1, source_target_pairs={{0,16},{8,24},{16,0},{24,8},{1,17},{9,25},{17,1},{25,9},{2,18},{10... | collective-permute-start | bytes 393224 | tf_op jit(solution)/shard_map/ppermute | solution.py:287
  81.3 15.9 %all-to-all-start.1 = ((bf16[8,8,1024]{2,1,0:T(8,128)(2,1)}), bf16[8,8,1024]{2,1,0:T(8,128)(2,1)S(1)}, u32[]{:S(2)}, u32[]{:S(2)}) async-start(bf16[8,8,1024]{2,1,0:T(8,128)(2,1)} %fusion.16), calls=%async_computation.1 | async-start | bytes 262144 | tf_op jit(solution)/shard_map/all_to_all | solution.py:34
  88.3 24.9 %collective-permute-start.19 = (bf16[256,1024]{1,0:T(8,128)(2,1)S(1)}, bf16[256,1024]{1,0:T(8,128)(2,1)S(1)}, u32[]{:S(2)}, u32[]{:S(2)}) collective-permute-start(bf16[256,1024]{1,0:T(8,128)(2,1)S(1)} %get-tuple-element.13), channel_id=1, source_target_pairs={{0,3},{1,0},{2,1},{3,2},{4,7},{5,4},{6,5},{7,6},{8,11},{9,8},{10,9... | collective-permute-start | bytes 1572872 | tf_op jit(solution)/shard_map/ppermute | solution.py:280
  88.9 14.7 %collective-permute-start.12 = (bf16[256,1024]{1,0:T(8,128)(2,1)S(1)}, bf16[256,1024]{1,0:T(8,128)(2,1)S(1)}, u32[]{:S(2)}, u32[]{:S(2)}) collective-permute-start(bf16[256,1024]{1,0:T(8,128)(2,1)S(1)} %get-tuple-element.12), channel_id=1, source_target_pairs={{0,1},{1,2},{2,3},{3,0},{4,5},{5,6},{6,7},{7,4},{8,9},{9,10},{10,1... | collective-permute-start | bytes 1572872 | tf_op jit(solution)/shard_map/ppermute | solution.py:279
  98.0 13.2 %all-to-all-start.2 = ((bf16[32,8,256]{2,1,0:T(8,128)(2,1)}), bf16[32,8,256]{2,1,0:T(8,128)(2,1)S(1)}, u32[]{:S(2)}, u32[]{:S(2)}) async-start(bf16[32,8,256]{2,1,0:T(8,128)(2,1)} %bitcast.9), calls=%async_computation.2 | async-start | bytes 262144 | tf_op jit(solution)/shard_map/all_to_all | solution.py:34
  102.7 19.1 %collective-permute-start.14 = (bf16[256,1024]{1,0:T(8,128)(2,1)S(1)}, bf16[256,1024]{1,0:T(8,128)(2,1)S(1)}, u32[]{:S(2)}, u32[]{:S(2)}) collective-permute-start(bf16[256,1024]{1,0:T(8,128)(2,1)S(1)} %get-tuple-element.12), channel_id=1, source_target_pairs={{0,3},{1,0},{2,1},{3,2},{4,7},{5,4},{6,5},{7,6},{8,11},{9,8},{10,9... | collective-permute-start | bytes 1572872 | tf_op jit(solution)/shard_map/ppermute | solution.py:284
  103.6 18.2 %collective-permute-start.13 = (bf16[256,1024]{1,0:T(8,128)(2,1)S(1)}, bf16[256,1024]{1,0:T(8,128)(2,1)}, u32[]{:S(2)}, u32[]{:S(2)}) collective-permute-start(bf16[256,1024]{1,0:T(8,128)(2,1)S(1)} %collective-permute-done.12), channel_id=1, source_target_pairs={{0,1},{1,2},{2,3},{3,0},{4,5},{5,6},{6,7},{7,4},{8,9},{9,10},{10,1... | collective-permute-start | bytes 1572872 | tf_op jit(solution)/shard_map/ppermute | solution.py:281
  111.3 7.7 %collective-permute-start.15 = (bf16[4,8,8,256]{3,2,1,0:T(8,128)(2,1)S(1)}, bf16[4,8,8,256]{3,2,1,0:T(8,128)(2,1)S(1)}, u32[]{:S(2)}, u32[]{:S(2)}) collective-permute-start(bf16[4,8,8,256]{3,2,1,0:T(8,128)(2,1)S(1)} %get-tuple-element.18), channel_id=1, source_target_pairs={{0,8},{8,16},{16,24},{24,0},{1,9},{9,17},{17,25},{25,1},{2,10},{10... | collective-permute-start | bytes 393224 | tf_op jit(solution)/shard_map/ppermute | solution.py:299
  111.4 9.6 %collective-permute-start.16 = (bf16[4,8,8,256]{3,2,1,0:T(8,128)(2,1)S(1)}, bf16[4,8,8,256]{3,2,1,0:T(8,128)(2,1)S(1)}, u32[]{:S(2)}, u32[]{:S(2)}) collective-permute-start(bf16[4,8,8,256]{3,2,1,0:T(8,128)(2,1)S(1)} %get-tuple-element.18), channel_id=1, source_target_pairs={{0,16},{8,24},{16,0},{24,8},{1,17},{9,25},{17,1},{25,9},{2,18},{10... | collective-permute-start | bytes 393224 | tf_op jit(solution)/shard_map/ppermute | solution.py:299
  113.3 7.7 %collective-permute-start.17 = (bf16[4,8,8,256]{3,2,1,0:T(8,128)(2,1)S(1)}, bf16[4,8,8,256]{3,2,1,0:T(8,128)(2,1)S(1)}, u32[]{:S(2)}, u32[]{:S(2)}) collective-permute-start(bf16[4,8,8,256]{3,2,1,0:T(8,128)(2,1)S(1)} %get-tuple-element.18), channel_id=1, source_target_pairs={{0,24},{8,0},{16,8},{24,16},{1,25},{9,1},{17,9},{25,17},{2,26},{10... | collective-permute-start | bytes 393224 | tf_op jit(solution)/shard_map/ppermute | solution.py:299
  118.9 9.3 %collective-permute-start.18 = (bf16[256,1024]{1,0:T(8,128)(2,1)S(1)}, bf16[256,1024]{1,0:T(8,128)(2,1)}, u32[]{:S(2)}, u32[]{:S(2)}) collective-permute-start(bf16[256,1024]{1,0:T(8,128)(2,1)S(1)} %get-tuple-element.13), channel_id=1, source_target_pairs={{0,1},{1,2},{2,3},{3,0},{4,5},{5,6},{6,7},{7,4},{8,9},{9,10},{10,1... | collective-permute-start | bytes 1572872 | tf_op jit(solution)/shard_map/ppermute | solution.py:283
  120.9 10.5 %collective-permute-start.20 = (bf16[256,1024]{1,0:T(8,128)(2,1)S(1)}, bf16[256,1024]{1,0:T(8,128)(2,1)}, u32[]{:S(2)}, u32[]{:S(2)}) collective-permute-start(bf16[256,1024]{1,0:T(8,128)(2,1)S(1)} %collective-permute-done.19), channel_id=1, source_target_pairs={{0,3},{1,0},{2,1},{3,2},{4,7},{5,4},{6,5},{7,6},{8,11},{9,8},{10,9... | collective-permute-start | bytes 1572872 | tf_op jit(solution)/shard_map/ppermute | solution.py:282
  121.1 10.3 %collective-permute-start.21 = (bf16[1024,256]{1,0:T(8,128)(2,1)S(1)}, bf16[1024,256]{1,0:T(8,128)(2,1)}, u32[]{:S(2)}, u32[]{:S(2)}) collective-permute-start(bf16[1024,256]{1,0:T(8,128)(2,1)S(1)} %bitcast.30), channel_id=1, source_target_pairs={{0,4},{4,0},{1,5},{5,1},{2,6},{6,2},{3,7},{7,3},{8,12},{12,8},{9,1... | collective-permute-start | bytes 1572872 | tf_op jit(solution)/shard_map/ppermute | solution.py:302
